TPU v7x, 32 devices: a whole 2x2x4 slice. The times are simulated.
32 devices in a mesh: dp: 2 (over core), row: 4 (over y, x), col: 4 (over z).
Axes of the slice: x: 2, y: 2, z: 4, core: 2. Of those that a mesh axis runs over, the one named last changes fastest.
Arguments:
- inputs: bfloat16 [2, 16, 4, 16, 2048], P('dp', 'row', None, None, 'col'), may hold values from -6 to 6
- up_weight: bfloat16 [2048, 4096], P(None, 'col'), may hold values from -0.1875 to 0.1875
- down_weight: bfloat16 [2048, 4096], P(None, 'col'), may hold values from -0.125 to 0.125
- kernel: float32 [125, 4096], P(None, 'col'), may hold values from -0.625 to 0.625
- cotangent: bfloat16 [2, 16, 4, 16, 2048], P('dp', 'row', None, None, 'col'), may hold values from -2 to 2
Outputs:
- block_output: bfloat16 [2, 16, 4, 16, 2048], P('dp', 'row', None, None, 'col')
- input_grad: bfloat16 [2, 16, 4, 16, 2048], P('dp', 'row', None, None, 'col')
- up_grad: bfloat16 [2048, 4096], P(('dp', 'row'), 'col')
- down_grad: bfloat16 [2048, 4096], P(('dp', 'row'), 'col')
- kernel_grad: float32 [125, 4096], P(None, 'col')
All inputs are finite; a program needn't handle non-finite values.
Results may differ from a plain program's by a relative error of at most 0.012.
Values may be sent and summed in bfloat16 or wider, within the bound.
A program may use at most 128 MiB of HBM per device.

v0:
```python
import jax
import jax.numpy as jnp
from jax import lax
from jax.sharding import PartitionSpec as P


def with_halo(shard, sides, width):
    for axis, dim in sides:
        peers, length = (lax.axis_size(axis), shard.shape[dim])
        up = [(i, (i + 1) % peers) for i in range(peers - 1)]
        down = [(j, i) for i, j in up]
        last = lax.slice_in_dim(shard, length - width, length, axis=dim)
        initial = lax.slice_in_dim(shard, 0, width, axis=dim)
        before = lax.ppermute(last, axis, up)
        after = lax.ppermute(initial, axis, down)
        shard = jnp.concatenate([before, shard, after], axis=dim)
    return shard


def depth_margin(field):
    extended = with_halo(field, (("row", 1),), 2)
    return jnp.pad(extended, ((0, 0), (0, 0), (2, 2), (2, 2), (0, 0)))


def stencil_sum(padded, kernel, mirror):
    planes = padded.shape[1] - 4
    tile_x = padded.shape[2] - 4
    tile_y = padded.shape[3] - 4
    result = jnp.zeros(padded.shape[:1] + (planes, tile_x, tile_y, padded.shape[4]), jnp.float32)
    for depth_step in range(5):
        for row_step in range(5):
            for col_step in range(5):
                first_z = depth_step + mirror * (4 - 2 * depth_step)
                first_x = row_step + mirror * (4 - 2 * row_step)
                first_y = col_step + mirror * (4 - 2 * col_step)
                window = padded[
                    :,
                    first_z : first_z + planes,
                    first_x : first_x + tile_x,
                    first_y : first_y + tile_y,
                    :,
                ]
                result = result + kernel[25 * depth_step + 5 * row_step + col_step] * window
    return result


def kernel_terms(padded, grad_field):
    planes = grad_field.shape[1]
    tile_x = grad_field.shape[2]
    tile_y = grad_field.shape[3]
    grad_wide = grad_field.astype(jnp.float32)
    rows_list = []
    for depth_step in range(5):
        for row_step in range(5):
            for col_step in range(5):
                window = padded[
                    :,
                    depth_step : depth_step + planes,
                    row_step : row_step + tile_x,
                    col_step : col_step + tile_y,
                    :,
                ]
                rows_list.append(jnp.sum(window * grad_wide, axis=(0, 1, 2, 3)))
    return jnp.stack(rows_list)


def column_sum(partial_value, field_shape):
    return lax.psum_scatter(
        partial_value.reshape(field_shape).astype(jnp.bfloat16),
        "col",
        scatter_dimension=4,
        tiled=True,
    ).astype(jnp.float32)


def spread_product(left_rows, right_rows):
    return lax.dot_general(
        left_rows, right_rows, (((0,), (0,)), ((), ())), preferred_element_type=jnp.float32
    )


def on_device(inputs, up_weight, down_weight, kernel, cotangent):
    states, planes, tile_x, tile_y, local_width = inputs.shape
    voxels = states * planes * tile_x * tile_y
    local_hidden = up_weight.shape[1]
    contract_last = (((1,), (1,)), ((), ()))
    input_rows, cotangent_rows = (
        lax.all_gather(inputs, "col", axis=4, tiled=True),
        lax.all_gather(cotangent, "col", axis=4, tiled=True),
    )
    full_width = input_rows.shape[4]
    field_shape = (states, planes, tile_x, tile_y, full_width)
    hidden_shape = (states, planes, tile_x, tile_y, local_hidden)
    flat_inputs = input_rows.reshape(voxels, full_width)
    hidden = jnp.dot(flat_inputs, up_weight, preferred_element_type=jnp.float32).astype(
        jnp.bfloat16
    )
    hidden_pad = depth_margin(hidden.reshape(hidden_shape))
    preact = stencil_sum(hidden_pad, kernel, 0)
    activation = jax.nn.silu(preact).astype(jnp.bfloat16)
    flat_act = activation.reshape(voxels, local_hidden)
    mixed_share = column_sum(
        lax.dot_general(flat_act, down_weight, contract_last, preferred_element_type=jnp.float32),
        field_shape,
    )
    block_output = (inputs.astype(jnp.float32) + mixed_share).astype(jnp.bfloat16)
    flat_cotangent = cotangent_rows.reshape(voxels, full_width)
    act_grad = jnp.dot(flat_cotangent, down_weight, preferred_element_type=jnp.float32).reshape(
        hidden_shape
    )
    logistic = jax.nn.sigmoid(preact)
    preact_grad = (act_grad * logistic * (1.0 + preact * (1.0 - logistic))).astype(jnp.bfloat16)
    grad_pad = depth_margin(preact_grad)
    hidden_grad = stencil_sum(grad_pad, kernel, 1).astype(jnp.bfloat16)
    kernel_grad = lax.psum(
        kernel_terms(hidden_pad, preact_grad).astype(jnp.bfloat16), ("dp", "row")
    ).astype(jnp.float32)
    flat_grad_hidden = hidden_grad.reshape(voxels, local_hidden)
    input_share = column_sum(
        lax.dot_general(
            flat_grad_hidden, up_weight, contract_last, preferred_element_type=jnp.float32
        ),
        field_shape,
    )
    input_grad = (cotangent.astype(jnp.float32) + input_share).astype(jnp.bfloat16)
    both_share = lax.psum_scatter(
        jnp.concatenate(
            [
                spread_product(flat_inputs, flat_grad_hidden),
                spread_product(flat_cotangent, flat_act),
            ],
            axis=1,
        ).astype(jnp.bfloat16),
        ("dp", "row"),
        scatter_dimension=0,
        tiled=True,
    ).astype(jnp.float32)
    up_share = both_share[:, :local_hidden]
    down_share = both_share[:, local_hidden:]
    up_grad = up_share.astype(jnp.bfloat16)
    down_grad = down_share.astype(jnp.bfloat16)
    return (block_output, input_grad, up_grad, down_grad, kernel_grad)


def solution(mesh):
    placed = (
        P("dp", "row", None, None, "col"),
        P(None, "col"),
        P(None, "col"),
        P(None, "col"),
        P("dp", "row", None, None, "col"),
    )
    return jax.shard_map(
        on_device,
        mesh=mesh,
        in_specs=placed,
        out_specs=(
            P("dp", "row", None, None, "col"),
            P("dp", "row", None, None, "col"),
            P(("dp", "row"), "col"),
            P(("dp", "row"), "col"),
            P(None, "col"),
        ),
        check_vma=False,
    )
```

profile of v0, /device:TPU:0, one launch (start us, length us, event | category | flops | bytes accessed | tf_op | source)
XLA Modules:
  0.0 385.0 jit_solution(17823461748566457241)
XLA Ops:
  8.7 1.3 fusion.328
  10.0 2.0 fusion.327
  12.0 1.9 fusion.326
  13.9 1.9 fusion.325
  15.9 2.0 fusion.324
  17.9 22.3 %all-gather.3.cloned.1.call-done = bf16[1,4,4,16,2048]{4,3,2,1,0:T(8,128)(2,1)} async-done(((bf16[1,4,4,16,512]{4,3,2,1,0:T(8,128)(2,1)}), bf16[1,4,4,16,2048]{4,3,2,1,0:T(8,128)(2,1)}) %all-gather.3.cloned.1.call-update) | async-done | bytes 1048592 | tf_op jit(solution)/shard_map/all_gather | solution.py:88
  40.2 3.8 convolution_convert_fusion
  45.8 4.7 %collective-permute-start = (bf16[1,2,4,16,1024]{4,3,2,1,0:T(8,128)(2,1)S(1)}, bf16[1,2,4,16,1024]{4,3,2,1,0:T(8,128)(2,1)S(1)}, u32[]{:S(2)}, u32[]{:S(2)}) collective-permute-start(bf16[1,2,4,16,1024]{4,3,2,1,0:T(8,128)(2,1)S(1)} %get-tuple-element.142), channel_id=1, source_target_pairs={{0,4},{4,8},{8,12},{1,5},{5,9},{9,13},{2,6},{6,10},{10,14},{3,7},{... | collective-permute-start | bytes 786440 | tf_op jit(solution)/shard_map/ppermute | solution.py:14
  51.7 1.4 fusion.329
  53.3 2.3 collective-permute-done.1
  57.1 28.9 %fusion.159 = f32[1,4,4,16,1024]{4,3,2,1,0:T(8,128)} fusion(bf16[1,4,4,16,1024]{4,3,2,1,0:T(8,128)(2,1)S(1)} %bitcast.210, f32[1024]{0:T(1024)S(1)} %bitcast.420, f32[1024]{0:T(1024)S(1)} %bitcast.422, f32[1024]{0:T(1024)} %bitcast.366, f32[1024]{0:T(1024)} %bitcast.368, f32[1024]{0:T(1024)} %bitcast.370, f32[1024]{0:T(1024)} %bitcast.372, ...), kind=kLoop, calls=%fused_computation.406 | loop fusion | flops 99090432 | bytes 65523712 | tf_op jit(solution)/shard_map/add | solution.py:43
  86.1 6.9 %fusion.303 = (bf16[1024]{0:T(1024)(128)(2,1)}, bf16[1024]{0:T(1024)(128)(2,1)}, bf16[1024]{0:T(1024)(128)(2,1)}, bf16[1024]{0:T(1024)(128)(2,1)}, bf16[1024]{0:...) fusion(bf16[1,8,8,20,1024]{4,3,2,1,0:T(8,128)(2,1)S(1)} %select, ...), kind=kOutput, calls=%fused_computation.550 | convolution fusion | flops 1086573568 | bytes 13658112 | tf_op jit(solution)/shard_map/dot_general | solution.py:108
  93.1 3.4 fusion.308
  96.5 3.4 fusion.309
  99.9 3.4 fusion.306
  103.3 3.4 fusion.304
  106.7 3.3 fusion.305
  110.0 3.4 fusion.307
  113.8 2.3 fusion.21
  175.0 10.6 %stack.629 = bf16[125,1024]{1,0:T(8,128)(2,1)} concatenate(bf16[1,1024]{1,0:T(2,128)(2,1)S(1)} %stack.504, bf16[1,1024]{1,0:T(2,128)(2,1)S(1)} %stack.505, bf16[1,1024]{1,0:T(2,128)(2,1)S(1)} %stack.506, bf16[1,1024]{1,0:T(2,128)(2,1)S(1)} %stack.507, bf16[1,1024]{1,0:T(2,128)(2,1)S(1)} %stack.508, bf16[1,1024]{1,0:T(2,128)(2,1)S(1)} %stack.509, bf16[1,1024]{1,0:T(2,128)(2,1)S(1)} %stack.510, ...), dimensions={0} | concatenate | bytes 512000 | tf_op jit(solution)/shard_map/stack | solution.py:64
  187.0 6.4 %collective-permute-start.2 = (bf16[1,2,4,16,1024]{4,3,2,1,0:T(8,128)(2,1)S(1)}, bf16[1,2,4,16,1024]{4,3,2,1,0:T(8,128)(2,1)S(1)}, u32[]{:S(2)}, u32[]{:S(2)}) collective-permute-start(bf16[1,2,4,16,1024]{4,3,2,1,0:T(8,128)(2,1)S(1)} %get-tuple-element.140), channel_id=1, source_target_pairs={{0,4},{4,8},{8,12},{1,5},{5,9},{9,13},{2,6},{6,10},{10,14},{3,7},{... | collective-permute-start | bytes 786440 | tf_op jit(solution)/shard_map/ppermute | solution.py:14
  193.5 4.5 %fusion.10 = bf16[2048,1024]{0,1:T(8,128)(2,1)} fusion(bf16[1,4,4,16,2048]{4,3,2,1,0:T(8,128)(2,1)} %all-gather.5.cloned.1.call-done, f32[1,4,4,16,1024]{4,3,2,1,0:T(8,128)S(1)} %copy-done.7), kind=kOutput, calls=%fused_computation.143 | convolution fusion | flops 1077149696 | bytes 6291456 | tf_op jit(solution)/shard_map/dot_general | solution.py:77
  200.0 30.2 %add_convert_fusion = bf16[1,4,4,16,1024]{4,3,2,1,0:T(8,128)(2,1)S(1)} fusion(bf16[1,4,4,16,1024]{4,3,2,1,0:T(8,128)(2,1)S(1)} %copy-done.1, bf16[1,2,4,16,1024]{4,3,2,1,0:T(8,128)(2,1)S(1)} %collective-permute-done.2, bf16[1,2,4,16,1024]{4,3,2,1,0:T(8,128)(2,1)S(1)} %collective-permute-done.3, bf16[1,8,8,20,1024]{4,3,2,1,0:T(8,128)(2,1)S(1)} %select_maximum_fusion, ...), kind=kLoop, calls=%fused_computation.560 | loop fusion | flops 99352576 | bytes 64999424 | tf_op jit(solution)/shard_map/convert_element_type | solution.py:114
  230.2 4.5 %fusion.18 = bf16[1,4,4,16,2048]{4,3,2,1,0:T(8,128)(2,1)} fusion(bf16[2048,1024]{1,0:T(8,128)(2,1)} %param.6, bf16[1,4,4,16,1024]{4,3,2,1,0:T(8,128)(2,1)S(1)} %add_convert_fusion), kind=kOutput, calls=%fused_computation.151 | convolution fusion | flops 1074266112 | bytes 5767168 | tf_op jit(solution)/shard_map/dot_general | solution.py:120
  234.8 4.5 %fusion.9 = bf16[2048,1024]{0,1:T(8,128)(2,1)} fusion(bf16[1,4,4,16,2048]{4,3,2,1,0:T(8,128)(2,1)} %all-gather.3.cloned.1.call-done, bf16[1,4,4,16,1024]{4,3,2,1,0:T(8,128)(2,1)S(1)} %add_convert_fusion), kind=kOutput, calls=%fused_computation.142 | convolution fusion | flops 1075838976 | bytes 5767168 | tf_op jit(solution)/shard_map/dot_general | solution.py:77
  239.3 8.4 %pad_maximum_fusion = bf16[2048,2048]{0,1:T(8,128)(2,1)} fusion(bf16[2048,1024]{0,1:T(8,128)(2,1)} %fusion.10, bf16[2048,1024]{0,1:T(8,128)(2,1)} %fusion.9), kind=kLoop, calls=%fused_computation.130 | loop fusion | flops 16777216 | bytes 16777216 | tf_op jit(solution)/shard_map/concatenate | solution.py:127
  247.7 1.8 convert_element_type.1202
  249.6 23.6 %reduce-scatter.4.cloned.1.call-done = bf16[1,4,4,16,512]{4,3,2,1,0:T(8,128)(2,1)} async-done(((bf16[1,4,4,16,2048]{4,3,2,1,0:T(8,128)(2,1)}), bf16[1,4,4,16,512]{4,3,2,1,0:T(8,128)(2,1)}) %reduce-scatter.4.cloned.1.call-update) | async-done | bytes 262160 | tf_op jit(solution)/shard_map/reduce_scatter | solution.py:68
  273.2 1.7 add_convert_fusion.2
  274.9 26.2 %reduce-scatter.6.cloned.1.call-done = bf16[1,4,4,16,512]{4,3,2,1,0:T(8,128)(2,1)} async-done(((bf16[1,4,4,16,2048]{4,3,2,1,0:T(8,128)(2,1)}), bf16[1,4,4,16,512]{4,3,2,1,0:T(8,128)(2,1)}) %reduce-scatter.6.cloned.1.call-update) | async-done | bytes 262160 | tf_op jit(solution)/shard_map/reduce_scatter | solution.py:68
  301.1 1.7 add_convert_fusion.1
  302.9 71.9 %reduce-scatter.8.cloned.1.call-done = bf16[256,2048]{0,1:T(8,128)(2,1)} async-done(((bf16[2048,2048]{0,1:T(8,128)(2,1)}), bf16[256,2048]{0,1:T(8,128)(2,1)}) %reduce-scatter.8.cloned.1.call-update) | async-done | bytes 1048592 | tf_op jit(solution)/shard_map/reduce_scatter | solution.py:126
  (465 shorter events, 69.6 us)
Async XLA Ops:
  7.2 33.1 %all-gather.3.cloned.1.call-start = ((), (), s32[]{:S(2)}) async-start(), calls=%async_computation.3 | async-start | bytes 1310720 | tf_op jit(solution)/shard_map/all_gather | solution.py:88
  7.9 78.2 %all-gather.5.cloned.1.call-start = ((), (), s32[]{:S(2)}) async-start(), calls=%async_computation.5 | async-start | bytes 1310720 | tf_op jit(solution)/shard_map/all_gather | solution.py:89
  8.6 239.1 %all-reduce.4.cloned.1.call-start = ((), (), s32[]{:S(2)}) async-start(), calls=%async_computation.8 | async-start | bytes 524288 | tf_op jit(solution)/shard_map/psum | solution.py:115
  44.5 11.1 %collective-permute-start.1 = (bf16[1,2,4,16,1024]{4,3,2,1,0:T(8,128)(2,1)S(1)}, bf16[1,2,4,16,1024]{4,3,2,1,0:T(8,128)(2,1)S(1)}, u32[]{:S(2)}, u32[]{:S(2)}) collective-permute-start(bf16[1,2,4,16,1024]{4,3,2,1,0:T(8,128)(2,1)S(1)} %get-tuple-element.141), channel_id=1, source_target_pairs={{4,0},{8,4},{12,8},{5,1},{9,5},{13,9},{6,2},{10,6},{14,10},{7,3},{... | collective-permute-start | bytes 786440 | tf_op jit(solution)/shard_map/ppermute | solution.py:15
  45.8 9.8 %collective-permute-start = (bf16[1,2,4,16,1024]{4,3,2,1,0:T(8,128)(2,1)S(1)}, bf16[1,2,4,16,1024]{4,3,2,1,0:T(8,128)(2,1)S(1)}, u32[]{:S(2)}, u32[]{:S(2)}) collective-permute-start(bf16[1,2,4,16,1024]{4,3,2,1,0:T(8,128)(2,1)S(1)} %get-tuple-element.142), channel_id=1, source_target_pairs={{0,4},{4,8},{8,12},{1,5},{5,9},{9,13},{2,6},{6,10},{10,14},{3,7},{... | collective-permute-start | bytes 786440 | tf_op jit(solution)/shard_map/ppermute | solution.py:14
  113.5 60.9 %copy-start.140 = (bf16[1024]{0:T(1024)(128)(2,1)S(1)}, bf16[1024]{0:T(1024)(128)(2,1)}, u32[]{:S(2)}) copy-start(bf16[1024]{0:T(1024)(128)(2,1)} %get-tuple-element.96) | copy-start | bytes 6148
  113.6 61.0 %copy-start.139 = (bf16[1024]{0:T(1024)(128)(2,1)S(1)}, bf16[1024]{0:T(1024)(128)(2,1)}, u32[]{:S(2)}) copy-start(bf16[1024]{0:T(1024)(128)(2,1)} %get-tuple-element.97) | copy-start | bytes 6148
  113.6 61.0 %copy-start.138 = (bf16[1024]{0:T(1024)(128)(2,1)S(1)}, bf16[1024]{0:T(1024)(128)(2,1)}, u32[]{:S(2)}) copy-start(bf16[1024]{0:T(1024)(128)(2,1)} %get-tuple-element.98) | copy-start | bytes 6148
  113.6 61.0 %copy-start.136 = (bf16[1024]{0:T(1024)(128)(2,1)S(1)}, bf16[1024]{0:T(1024)(128)(2,1)}, u32[]{:S(2)}) copy-start(bf16[1024]{0:T(1024)(128)(2,1)} %get-tuple-element.99) | copy-start | bytes 6148
  113.6 61.0 %copy-start.137 = (bf16[1024]{0:T(1024)(128)(2,1)S(1)}, bf16[1024]{0:T(1024)(128)(2,1)}, u32[]{:S(2)}) copy-start(bf16[1024]{0:T(1024)(128)(2,1)} %get-tuple-element.47) | copy-start | bytes 6148
  113.6 61.0 %copy-start.135 = (bf16[1024]{0:T(1024)(128)(2,1)S(1)}, bf16[1024]{0:T(1024)(128)(2,1)}, u32[]{:S(2)}) copy-start(bf16[1024]{0:T(1024)(128)(2,1)} %get-tuple-element.48) | copy-start | bytes 6148
  113.6 61.0 %copy-start.134 = (bf16[1024]{0:T(1024)(128)(2,1)S(1)}, bf16[1024]{0:T(1024)(128)(2,1)}, u32[]{:S(2)}) copy-start(bf16[1024]{0:T(1024)(128)(2,1)} %get-tuple-element.49) | copy-start | bytes 6148
  113.6 61.0 %copy-start.133 = (bf16[1024]{0:T(1024)(128)(2,1)S(1)}, bf16[1024]{0:T(1024)(128)(2,1)}, u32[]{:S(2)}) copy-start(bf16[1024]{0:T(1024)(128)(2,1)} %get-tuple-element.50) | copy-start | bytes 6148
  113.6 61.0 %copy-start.132 = (bf16[1024]{0:T(1024)(128)(2,1)S(1)}, bf16[1024]{0:T(1024)(128)(2,1)}, u32[]{:S(2)}) copy-start(bf16[1024]{0:T(1024)(128)(2,1)} %get-tuple-element.51) | copy-start | bytes 6148
  113.6 61.1 %copy-start.131 = (bf16[1024]{0:T(1024)(128)(2,1)S(1)}, bf16[1024]{0:T(1024)(128)(2,1)}, u32[]{:S(2)}) copy-start(bf16[1024]{0:T(1024)(128)(2,1)} %get-tuple-element.52) | copy-start | bytes 6148
  113.7 61.1 %copy-start.130 = (bf16[1024]{0:T(1024)(128)(2,1)S(1)}, bf16[1024]{0:T(1024)(128)(2,1)}, u32[]{:S(2)}) copy-start(bf16[1024]{0:T(1024)(128)(2,1)} %get-tuple-element.53) | copy-start | bytes 6148
  113.7 61.1 %copy-start.129 = (bf16[1024]{0:T(1024)(128)(2,1)S(1)}, bf16[1024]{0:T(1024)(128)(2,1)}, u32[]{:S(2)}) copy-start(bf16[1024]{0:T(1024)(128)(2,1)} %get-tuple-element.54) | copy-start | bytes 6148
  113.7 61.1 %copy-start.128 = (bf16[1024]{0:T(1024)(128)(2,1)S(1)}, bf16[1024]{0:T(1024)(128)(2,1)}, u32[]{:S(2)}) copy-start(bf16[1024]{0:T(1024)(128)(2,1)} %get-tuple-element.55) | copy-start | bytes 6148
  113.7 61.1 %copy-start.127 = (bf16[1024]{0:T(1024)(128)(2,1)S(1)}, bf16[1024]{0:T(1024)(128)(2,1)}, u32[]{:S(2)}) copy-start(bf16[1024]{0:T(1024)(128)(2,1)} %get-tuple-element.56) | copy-start | bytes 6148
  113.7 61.1 %copy-start.126 = (bf16[1024]{0:T(1024)(128)(2,1)S(1)}, bf16[1024]{0:T(1024)(128)(2,1)}, u32[]{:S(2)}) copy-start(bf16[1024]{0:T(1024)(128)(2,1)} %get-tuple-element.57) | copy-start | bytes 6148
  113.7 61.1 %copy-start.125 = (bf16[1024]{0:T(1024)(128)(2,1)S(1)}, bf16[1024]{0:T(1024)(128)(2,1)}, u32[]{:S(2)}) copy-start(bf16[1024]{0:T(1024)(128)(2,1)} %get-tuple-element.58) | copy-start | bytes 6148
  113.7 61.2 %copy-start.124 = (bf16[1024]{0:T(1024)(128)(2,1)S(1)}, bf16[1024]{0:T(1024)(128)(2,1)}, u32[]{:S(2)}) copy-start(bf16[1024]{0:T(1024)(128)(2,1)} %get-tuple-element.59) | copy-start | bytes 6148
  113.7 61.2 %copy-start.123 = (bf16[1024]{0:T(1024)(128)(2,1)S(1)}, bf16[1024]{0:T(1024)(128)(2,1)}, u32[]{:S(2)}) copy-start(bf16[1024]{0:T(1024)(128)(2,1)} %get-tuple-element.60) | copy-start | bytes 6148
  113.7 61.2 %copy-start.122 = (bf16[1024]{0:T(1024)(128)(2,1)S(1)}, bf16[1024]{0:T(1024)(128)(2,1)}, u32[]{:S(2)}) copy-start(bf16[1024]{0:T(1024)(128)(2,1)} %get-tuple-element.61) | copy-start | bytes 6148
  113.7 61.2 %copy-start.121 = (bf16[1024]{0:T(1024)(128)(2,1)S(1)}, bf16[1024]{0:T(1024)(128)(2,1)}, u32[]{:S(2)}) copy-start(bf16[1024]{0:T(1024)(128)(2,1)} %get-tuple-element.62) | copy-start | bytes 6148
  113.8 61.2 %copy-start.120 = (bf16[1024]{0:T(1024)(128)(2,1)S(1)}, bf16[1024]{0:T(1024)(128)(2,1)}, u32[]{:S(2)}) copy-start(bf16[1024]{0:T(1024)(128)(2,1)} %get-tuple-element.63) | copy-start | bytes 6148
  116.0 77.5 %copy-start.7 = (f32[1,4,4,16,1024]{4,3,2,1,0:T(8,128)S(1)}, f32[1,4,4,16,1024]{4,3,2,1,0:T(8,128)}, u32[]{:S(2)}) copy-start(f32[1,4,4,16,1024]{4,3,2,1,0:T(8,128)} %fusion.159) | copy-start | bytes 3145732
  185.6 87.5 %reduce-scatter.4.cloned.1.call-start = ((), (), s32[]{:S(2)}) async-start(), calls=%async_computation.4 | async-start | bytes 1310720 | tf_op jit(solution)/shard_map/reduce_scatter | solution.py:68
  185.7 12.7 %collective-permute-start.3 = (bf16[1,2,4,16,1024]{4,3,2,1,0:T(8,128)(2,1)S(1)}, bf16[1,2,4,16,1024]{4,3,2,1,0:T(8,128)(2,1)S(1)}, u32[]{:S(2)}, u32[]{:S(2)}) collective-permute-start(bf16[1,2,4,16,1024]{4,3,2,1,0:T(8,128)(2,1)S(1)} %get-tuple-element.139), channel_id=1, source_target_pairs={{4,0},{8,4},{12,8},{5,1},{9,5},{13,9},{6,2},{10,6},{14,10},{7,3},{... | collective-permute-start | bytes 786440 | tf_op jit(solution)/shard_map/ppermute | solution.py:15
  187.0 11.4 %collective-permute-start.2 = (bf16[1,2,4,16,1024]{4,3,2,1,0:T(8,128)(2,1)S(1)}, bf16[1,2,4,16,1024]{4,3,2,1,0:T(8,128)(2,1)S(1)}, u32[]{:S(2)}, u32[]{:S(2)}) collective-permute-start(bf16[1,2,4,16,1024]{4,3,2,1,0:T(8,128)(2,1)S(1)} %get-tuple-element.140), channel_id=1, source_target_pairs={{0,4},{4,8},{8,12},{1,5},{5,9},{9,13},{2,6},{6,10},{10,14},{3,7},{... | collective-permute-start | bytes 786440 | tf_op jit(solution)/shard_map/ppermute | solution.py:14
  193.5 107.7 %reduce-scatter.6.cloned.1.call-start = ((), (), s32[]{:S(2)}) async-start(), calls=%async_computation.6 | async-start | bytes 1310720 | tf_op jit(solution)/shard_map/reduce_scatter | solution.py:68
  234.8 140.0 %reduce-scatter.8.cloned.1.call-start = ((), (), s32[]{:S(2)}) async-start(), calls=%async_computation.7 | async-start | bytes 9437184 | tf_op jit(solution)/shard_map/reduce_scatter | solution.py:126
  (134 other events, 1667.5 us)
Sparse Core Ops, SparseCore 0:
  9.6 30.6 all-gather.2
  41.8 27.4 all-gather.4
  185.8 58.5 all-reduce.3
  246.6 26.5 reduce-scatter.3
  275.3 25.7 reduce-scatter.5
  304.9 69.9 reduce-scatter.7
where the time goes:
time: 388 us; the launch traced here: 385 us
  waiting for transfers between devices  148 us (38%)
  other arithmetic  95.6 us (25%)
  local copies, waits for them, and re-layouts  84.1 us (22%)
  matrix products  26.5 us (7%)
  between operations  16.9 us (4%)
  starting transfers between devices  14 us (4%)
    reduce_scatter x1, waiting for transfers between devices, on_device(): lax.psum_scatter(jnp.concatenate([spread_product(flat_inputs, flat_grad_h...  71.9 us
    another operation x126, local copies, waits for them, and re-layouts, kernel_terms(): return jnp.stack(rows_list)  68.4 us
    reduce_scatter x2, waiting for transfers between devices, column_sum(): lax.psum_scatter(partial_value.reshape(field_shape).astype(jnp.bfloat16),...  49.8 us
    convert_element_type x1, other arithmetic, on_device(): hidden_grad = stencil_sum(grad_pad, kernel, 1).astype(jnp.bfloat16)  30.2 us
    add x1, other arithmetic, stencil_sum(): result = result + kernel[25 * depth_step + 5 * row_step + col_step] * window  28.9 us
    all_gather x1, waiting for transfers between devices, on_device(): lax.all_gather(inputs, 'col', axis=4, tiled=True)  22.3 us
    reduce_sum x7, other arithmetic, kernel_terms(): rows_list.append(jnp.sum(window * grad_wide, axis=(0, 1, 2, 3)))  20.7 us
    slice x7, local copies, waits for them, and re-layouts, stencil_sum(): result = result + kernel[25 * depth_step + 5 * row_step + col_step] * window  11.7 us
  transfers between devices with their start and end apart: 10, of which 5 were waited for; matrix products, arithmetic and copies ran while one was open for 27% of the time, Pallas kernels for 0%

commit v1 on v0

v1 whole, which is shorter than its diff:
```python
import functools

import jax
import jax.numpy as jnp
from jax import lax
from jax.experimental import pallas as pl
from jax.experimental.pallas import tpu as pltpu
from jax.sharding import PartitionSpec as P

LANES = 128


def lane_block(index):
    return pl.ds(pl.multiple_of(index * LANES, LANES), LANES)


def clear_windows(win):
    halves, depth, tile_x, _, lanes = win.shape
    zeros = jnp.zeros((8, lanes), jnp.float32)
    for z in range(depth):
        for x in range(tile_x):
            win[0, z, x, 0:8] = zeros
            win[halves - 1, z, x, 16:24] = zeros


def fill_windows(win, field, cols):
    halves, depth, tile_x, _, _ = win.shape
    for z in range(depth):
        for x in range(tile_x):
            line = field[z, x, :, cols].astype(jnp.float32)
            for h in range(halves):
                for part in range(3):
                    first = 8 * (h + part - 1)
                    if 0 <= first < 8 * halves:
                        win[h, z, x, 8 * part : 8 * part + 8] = line[first : first + 8]


def pairs(source_z, source_x, planes, tile_x):
    for a in range(5):
        z = source_z - a
        if 0 <= z < planes:
            for b in range(5):
                x = source_x - b + 2
                if 0 <= x < tile_x:
                    yield a, b, z, x


def stencil_half(win, half, kernel, cols, mirror, planes, tile_x):
    accs = [[None] * tile_x for _ in range(planes)]
    for c in range(5):
        taps = {}
        for a in range(5):
            for b in range(5):
                t = 25 * a + 5 * b + c
                t = 124 - t if mirror else t
                taps[a, b] = jnp.broadcast_to(kernel[t : t + 1, cols], (8, LANES))
        for sz in range(planes + 4):
            for sx in range(tile_x):
                cells = win[half, sz, sx, 6 + c : 14 + c]
                for a, b, z, x in pairs(sz, sx, planes, tile_x):
                    term = taps[a, b] * cells
                    accs[z][x] = term if accs[z][x] is None else accs[z][x] + term
    return accs


def tap_sums(win, grad, cols, planes, tile_x, halves, store):
    for c in range(5):
        def one_half(half, sums):
            sums = list(sums)
            rows = pl.ds(pl.multiple_of(half * 8, 8), 8)
            grads = [[grad[z, x, rows, :] for x in range(tile_x)] for z in range(planes)]
            for sz in range(planes + 4):
                for sx in range(tile_x):
                    cells = win[half, sz, sx, 6 + c : 14 + c]
                    for a, b, z, x in pairs(sz, sx, planes, tile_x):
                        sums[5 * a + b] = sums[5 * a + b] + cells * grads[z][x]
            return tuple(sums)

        sums = lax.fori_loop(0, halves, one_half, (jnp.zeros((8, LANES), jnp.float32),) * 25)
        for ab in range(25):
            store(5 * ab + c, jnp.sum(sums[ab], axis=0, keepdims=True))


def forward_kernel(field, kernel, out, win):
    planes, tile_x = out.shape[:2]
    halves = win.shape[0]
    clear_windows(win)

    @pl.loop(0, out.shape[3] // LANES)
    def _(block):
        cols = lane_block(block)
        fill_windows(win, field, cols)

        @pl.loop(0, halves)
        def _(half):
            rows = pl.ds(pl.multiple_of(half * 8, 8), 8)
            accs = stencil_half(win, half, kernel, cols, False, planes, tile_x)
            for z in range(planes):
                for x in range(tile_x):
                    out[z, x, rows, cols] = accs[z][x]


def backward_kernel(field, kernel, out, win, tmp):
    planes, tile_x = out.shape[:2]
    halves = win.shape[0]
    clear_windows(win)

    @pl.loop(0, out.shape[3] // LANES)
    def _(block):
        cols = lane_block(block)
        fill_windows(win, field, cols)

        @pl.loop(0, halves)
        def _(half):
            rows = pl.ds(pl.multiple_of(half * 8, 8), 8)
            accs = stencil_half(win, half, kernel, cols, True, planes, tile_x)
            for z in range(planes):
                for x in range(tile_x):
                    tmp[z, x, rows, :] = accs[z][x]

        for z in range(planes):
            for x in range(tile_x):
                out[z, x, :, cols] = tmp[z, x].astype(out.dtype)


def taps_kernel(field, grad, out, win, tmp):
    planes, tile_x = grad.shape[:2]
    halves = win.shape[0]
    clear_windows(win)

    @pl.loop(0, out.shape[1] // LANES)
    def _(block):
        cols = lane_block(block)
        fill_windows(win, field, cols)
        for z in range(planes):
            for x in range(tile_x):
                tmp[z, x] = grad[z, x, :, cols].astype(jnp.float32)

        def store(t, row):
            out[t : t + 1, cols] = row

        tap_sums(win, tmp, cols, planes, tile_x, halves, store)


def call(body, out_shape, shape, scratch_tmp, args):
    planes, tile_x, tile_y, _ = shape
    scratch = [pltpu.VMEM((tile_y // 8, planes + 4, tile_x, 24, LANES), jnp.float32)]
    if scratch_tmp:
        scratch.append(pltpu.VMEM((planes, tile_x, tile_y, LANES), jnp.float32))
    return pl.pallas_call(
        body,
        out_shape=out_shape,
        in_specs=[pl.BlockSpec(memory_space=pltpu.VMEM)] * len(args),
        out_specs=pl.BlockSpec(memory_space=pltpu.VMEM),
        scratch_shapes=scratch,
        compiler_params=pltpu.CompilerParams(vmem_limit_bytes=24 << 20),
        cost_estimate=pl.CostEstimate(flops=10**10, bytes_accessed=3 * 10**6, transcendentals=0),
    )(*args)


def with_halo(shard, width):
    peers, length = (lax.axis_size("row"), shard.shape[0])
    up = [(i, (i + 1) % peers) for i in range(peers - 1)]
    down = [(j, i) for i, j in up]
    before = lax.ppermute(lax.slice_in_dim(shard, length - width, length, axis=0), "row", up)
    after = lax.ppermute(lax.slice_in_dim(shard, 0, width, axis=0), "row", down)
    return jnp.concatenate([before, shard, after], axis=0)


def column_sum(partial_value, field_shape):
    return lax.psum_scatter(
        partial_value.reshape(field_shape).astype(jnp.bfloat16),
        "col",
        scatter_dimension=4,
        tiled=True,
    ).astype(jnp.float32)


def spread_product(left_rows, right_rows):
    product = lax.dot_general(
        left_rows, right_rows, (((0,), (0,)), ((), ())), preferred_element_type=jnp.float32
    ).astype(jnp.bfloat16)
    return lax.psum_scatter(product, ("dp", "row"), scatter_dimension=0, tiled=True)


def on_device(inputs, up_weight, down_weight, kernel, cotangent):
    states, planes, tile_x, tile_y, _ = inputs.shape
    voxels = planes * tile_x * tile_y
    local_hidden = up_weight.shape[1]
    contract_last = (((1,), (1,)), ((), ()))
    input_rows = lax.all_gather(inputs, "col", axis=4, tiled=True)
    cotangent_rows = lax.all_gather(cotangent, "col", axis=4, tiled=True)
    full_width = input_rows.shape[4]
    field_shape = (states, planes, tile_x, tile_y, full_width)
    shape = (planes, tile_x, tile_y, local_hidden)
    flat_inputs = input_rows.reshape(voxels, full_width)
    hidden = jnp.dot(flat_inputs, up_weight, preferred_element_type=jnp.float32)
    hidden_ext = with_halo(hidden.astype(jnp.bfloat16).reshape(shape), 2)
    preact = call(forward_kernel, jax.ShapeDtypeStruct(shape, jnp.float32), shape, False, (hidden_ext, kernel))
    activation = jax.nn.silu(preact).astype(jnp.bfloat16)
    flat_act = activation.reshape(voxels, local_hidden)
    flat_cotangent = cotangent_rows.reshape(voxels, full_width)
    down_grad = spread_product(flat_cotangent, flat_act)
    mixed_share = column_sum(
        lax.dot_general(flat_act, down_weight, contract_last, preferred_element_type=jnp.float32),
        field_shape,
    )
    block_output = (inputs.astype(jnp.float32) + mixed_share).astype(jnp.bfloat16)
    act_grad = jnp.dot(flat_cotangent, down_weight, preferred_element_type=jnp.float32).reshape(shape)
    logistic = jax.nn.sigmoid(preact)
    preact_grad = (act_grad * logistic * (1.0 + preact * (1.0 - logistic))).astype(jnp.bfloat16)
    grad_ext = with_halo(preact_grad, 2)
    kernel_grad = call(
        taps_kernel, jax.ShapeDtypeStruct(kernel.shape, jnp.float32), shape, True, (hidden_ext, preact_grad)
    )
    kernel_grad = lax.psum(kernel_grad.astype(jnp.bfloat16), ("dp", "row")).astype(jnp.float32)
    hidden_grad = call(
        backward_kernel, jax.ShapeDtypeStruct(shape, jnp.bfloat16), shape, True, (grad_ext, kernel)
    )
    flat_grad_hidden = hidden_grad.reshape(voxels, local_hidden)
    up_grad = spread_product(flat_inputs, flat_grad_hidden)
    input_share = column_sum(
        lax.dot_general(
            flat_grad_hidden, up_weight, contract_last, preferred_element_type=jnp.float32
        ),
        field_shape,
    )
    input_grad = (cotangent.astype(jnp.float32) + input_share).astype(jnp.bfloat16)
    return (block_output, input_grad, up_grad, down_grad, kernel_grad)


def solution(mesh):
    placed = (
        P("dp", "row", None, None, "col"),
        P(None, "col"),
        P(None, "col"),
        P(None, "col"),
        P("dp", "row", None, None, "col"),
    )
    return jax.shard_map(
        on_device,
        mesh=mesh,
        in_specs=placed,
        out_specs=(
            P("dp", "row", None, None, "col"),
            P("dp", "row", None, None, "col"),
            P(("dp", "row"), "col"),
            P(("dp", "row"), "col"),
            P(None, "col"),
        ),
        check_vma=False,
    )
```

time: 388 us -> 319 us (0.82)
  other arithmetic: 95.6 us -> 7.33 us
  waiting for transfers between devices: 148 us -> 234 us
  local copies, waits for them, and re-layouts: 84.1 us -> 4.19 us
  Pallas kernels: 0 us -> 26 us
  matrix products: 26.5 us -> 22.3 us
    another operation x126 -> x0, local copies, waits for them, and re-layouts: 68.4 us -> none  [kernel_terms(): return jnp.stack(rows_list)]
    reduce_scatter x1 -> x2, waiting for transfers between devices: 71.9 us -> 105 us  [spread_product(): lax.psum_scatter(product, ('dp', 'row'), scatter_dimension=0, tiled=True)]
    add x1 -> x0, other arithmetic: 28.9 us -> none  [stencil_sum(): result = result + kernel[25 * depth_step + 5 * row_step + col_step] * window]
    convert_element_type x2 -> x3, other arithmetic: 32.1 us -> 3.61 us  [the longest x1 1.79 us: on_device(): lax.psum(kernel_grad.astype(jnp.bfloat16), ('dp', 'row'))]
    pallas_call x0 -> x3, Pallas kernels: none -> 26 us  [call(): pl.pallas_call(body, out_shape=out_shape, in_specs=[pl.BlockSpec(memory_s...]
    all_gather x2, waiting for transfers between devices: 22.3 us -> 44.5 us  [the longest x1 32.3 us: on_device(): input_rows = lax.all_gather(inputs, 'col', axis=4, tiled=True)]
    reduce_sum x7 -> x0, other arithmetic: 20.7 us -> none  [kernel_terms(): rows_list.append(jnp.sum(window * grad_wide, axis=(0, 1, 2, 3)))]
    ppermute x4, waiting for transfers between devices: 2.29 us -> 17.4 us  [the longest x2 12.7 us: with_halo(): after = lax.ppermute(lax.slice_in_dim(shard, 0, width, axis=0), 'row', down)]
  transfers between devices with their start and end apart: 10 -> 11, of which waited for: 5 -> 10; matrix products, arithmetic and copies ran while one was open for 27% -> 7% of each run, Pallas kernels for 0% -> 6%
where the time goes in v1:
time: 319 us
  waiting for transfers between devices  234 us (73%)
  Pallas kernels  26 us (8%)
  matrix products  22.3 us (7%)
  between operations  14.3 us (4%)
  starting transfers between devices  10.8 us (3%)
  other arithmetic  7.33 us (2%)
  local copies, waits for them, and re-layouts  4.19 us (1%)
    reduce_scatter x2, waiting for transfers between devices, spread_product(): lax.psum_scatter(product, ('dp', 'row'), scatter_dimension=0, tiled=True)  105 us
    reduce_scatter x2, waiting for transfers between devices, column_sum(): lax.psum_scatter(partial_value.reshape(field_shape).astype(jnp.bfloat16),...  53.2 us
    all_gather x1, waiting for transfers between devices, on_device(): input_rows = lax.all_gather(inputs, 'col', axis=4, tiled=True)  32.3 us
    pallas_call x3, Pallas kernels, call(): pl.pallas_call(body, out_shape=out_shape, in_specs=[pl.BlockSpec(memory_s...  26 us
    psum x1, waiting for transfers between devices, on_device(): lax.psum(kernel_grad.astype(jnp.bfloat16), ('dp', 'row'))  13.2 us
    ppermute x2, waiting for transfers between devices, with_halo(): after = lax.ppermute(lax.slice_in_dim(shard, 0, width, axis=0), 'row', down)  12.7 us
    all_gather x1, waiting for transfers between devices, on_device(): cotangent_rows = lax.all_gather(cotangent, 'col', axis=4, tiled=True)  12.2 us
    ppermute x2, starting transfers between devices, with_halo(): lax.ppermute(lax.slice_in_dim(shard, length - width, length, axis=0), 'ro...  7.95 us
  transfers between devices with their start and end apart: 11, of which 10 were waited for; matrix products, arithmetic and copies ran while one was open for 7% of the time, Pallas kernels for 6%

profile of v1, /device:TPU:0, one launch (start us, length us, event | category | flops | bytes accessed | tf_op | source)
XLA Modules:
  0.0 318.7 jit_solution(9205562752040877835)
XLA Ops:
  7.2 0.7 all-gather.3.cloned.1.call-update
  7.9 32.3 %all-gather.3.cloned.1.call-done = bf16[1,4,4,16,2048]{4,3,2,1,0:T(8,128)(2,1)} async-done(((bf16[1,4,4,16,512]{4,3,2,1,0:T(8,128)(2,1)}), bf16[1,4,4,16,2048]{4,3,2,1,0:T(8,128)(2,1)}) %all-gather.3.cloned.1.call-update) | async-done | bytes 1048592 | tf_op jit(solution)/shard_map/all_gather | solution.py:191
  40.2 3.8 %convolution_convert_fusion = bf16[256,1024]{1,0:T(8,128)(2,1)S(1)} fusion(bf16[256,2048]{1,0:T(8,128)(2,1)} %bitcast.55, bf16[2048,1024]{1,0:T(8,128)(2,1)} %param.6), kind=kOutput, calls=%fused_computation.13 | convolution fusion | flops 1074003968 | bytes 5767168 | tf_op jit(solution)/shard_map/dot_general | solution.py:197
  44.1 1.3 collective-permute-start.1
  45.4 4.6 %collective-permute-start = (bf16[2,4,16,1024]{3,2,1,0:T(8,128)(2,1)S(1)}, bf16[2,4,16,1024]{3,2,1,0:T(8,128)(2,1)S(1)}, u32[]{:S(2)}, u32[]{:S(2)}) collective-permute-start(bf16[2,4,16,1024]{3,2,1,0:T(8,128)(2,1)S(1)} %bitcast.58), channel_id=1, source_target_pairs={{0,4},{4,8},{8,12},{1,5},{5,9},{9,13},{2,6},{6,10},{10,14},{3,7},{... | collective-permute-start | bytes 786440 | tf_op jit(solution)/shard_map/ppermute | solution.py:165
  50.0 5.2 %collective-permute-done.1 = bf16[2,4,16,1024]{3,2,1,0:T(8,128)(2,1)S(1)} collective-permute-done((bf16[2,4,16,1024]{3,2,1,0:T(8,128)(2,1)S(1)}, bf16[2,4,16,1024]{3,2,1,0:T(8,128)(2,1)S(1)}, u32[]{:S(2)}, u32[]{:S(2)}) %collective-permute-start.1) | collective-permute-done | bytes 262176 | tf_op jit(solution)/shard_map/ppermute | solution.py:166
  55.2 0.1 pad_maximum_fusion.field
  55.3 8.9 %shard_map.92 = f32[4,4,16,1024]{3,2,1,0:T(8,128)S(1)} custom-call(bf16[8,4,16,1024]{3,2,1,0:T(8,128)(2,1)S(1)} %pad_maximum_fusion.field, f32[125,1024]{1,0:T(8,128)S(1)} %copy-done), custom_call_target="tpu_custom_call" | custom-call | flops 10000000000 | bytes 3000000 | tf_op jit(solution)/shard_map/pallas_call | solution.py:150
  64.3 1.1 multiply_convert_fusion.1
  65.3 12.2 %all-gather.5.cloned.1.call-done = bf16[1,4,4,16,2048]{4,3,2,1,0:T(8,128)(2,1)} async-done(((bf16[1,4,4,16,512]{4,3,2,1,0:T(8,128)(2,1)}), bf16[1,4,4,16,2048]{4,3,2,1,0:T(8,128)(2,1)}) %all-gather.5.cloned.1.call-update) | async-done | bytes 1048592 | tf_op jit(solution)/shard_map/all_gather | solution.py:192
  77.5 3.9 %multiply_convert_fusion.grad = bf16[4,4,16,1024]{3,2,1,0:T(8,128)(2,1)S(1)} fusion(f32[4,4,16,1024]{3,2,1,0:T(8,128)S(1)} %shard_map.92, bf16[2048,1024]{1,0:T(8,128)(2,1)} %param.7, bf16[1,4,4,16,2048]{4,3,2,1,0:T(8,128)(2,1)} %all-gather.5.cloned.1.call-done), kind=kOutput, calls=%fused_computation.17 | convolution fusion | flops 1076101120 | bytes 6815744 | tf_op jit(solution)/shard_map/dot_general | solution.py:209
  81.5 8.1 %shard_map.94 = f32[125,1024]{1,0:T(8,128)S(1)} custom-call(bf16[8,4,16,1024]{3,2,1,0:T(8,128)(2,1)S(1)} %pad_maximum_fusion.field, bf16[4,4,16,1024]{3,2,1,0:T(8,128)(2,1)S(1)} %multiply_convert_fusion.grad), custom_call_target="tpu_custom_call" | custom-call | flops 10000000000 | bytes 3000000 | tf_op jit(solution)/shard_map/pallas_call | solution.py:150
  89.6 0.7 convert_element_type.74
  90.4 4.5 %fusion.15 = bf16[1,4,4,16,2048]{4,3,2,1,0:T(8,128)(2,1)} fusion(bf16[4,4,16,1024]{3,2,1,0:T(8,128)(2,1)S(1)} %copy-done.1, bf16[2048,1024]{1,0:T(8,128)(2,1)} %param.7), kind=kOutput, calls=%fused_computation.11 | convolution fusion | flops 1074266112 | bytes 5767168 | tf_op jit(solution)/shard_map/dot_general | solution.py:205
  95.0 3.4 %collective-permute-start.2 = (bf16[2,4,16,1024]{3,2,1,0:T(8,128)(2,1)S(1)}, bf16[2,4,16,1024]{3,2,1,0:T(8,128)(2,1)S(1)}, u32[]{:S(2)}, u32[]{:S(2)}) collective-permute-start(bf16[2,4,16,1024]{3,2,1,0:T(8,128)(2,1)S(1)} %get-tuple-element.10), channel_id=1, source_target_pairs={{0,4},{4,8},{8,12},{1,5},{5,9},{9,13},{2,6},{6,10},{10,14},{3,7},{... | collective-permute-start | bytes 786440 | tf_op jit(solution)/shard_map/ppermute | solution.py:165
  98.4 1.3 collective-permute-start.3
  99.7 4.7 %collective-permute-done.2 = bf16[2,4,16,1024]{3,2,1,0:T(8,128)(2,1)S(1)} collective-permute-done((bf16[2,4,16,1024]{3,2,1,0:T(8,128)(2,1)S(1)}, bf16[2,4,16,1024]{3,2,1,0:T(8,128)(2,1)S(1)}, u32[]{:S(2)}, u32[]{:S(2)}) %collective-permute-start.2) | collective-permute-done | bytes 262176 | tf_op jit(solution)/shard_map/ppermute | solution.py:165
  104.4 7.5 %collective-permute-done.3 = bf16[2,4,16,1024]{3,2,1,0:T(8,128)(2,1)S(1)} collective-permute-done((bf16[2,4,16,1024]{3,2,1,0:T(8,128)(2,1)S(1)}, bf16[2,4,16,1024]{3,2,1,0:T(8,128)(2,1)S(1)}, u32[]{:S(2)}, u32[]{:S(2)}) %collective-permute-start.3) | collective-permute-done | bytes 262176 | tf_op jit(solution)/shard_map/ppermute | solution.py:166
  112.1 9.0 %shard_map.93 = bf16[4,4,16,1024]{3,2,1,0:T(8,128)(2,1)S(1)} custom-call(bf16[8,4,16,1024]{3,2,1,0:T(8,128)(2,1)S(1)} %pad_maximum_fusion.1.field, f32[125,1024]{1,0:T(8,128)S(1)} %copy-done), custom_call_target="tpu_custom_call" | custom-call | flops 10000000000 | bytes 3000000 | tf_op jit(solution)/shard_map/pallas_call | solution.py:150
  121.2 2.3 fusion.12
  123.5 4.6 %convert_bitcast_fusion = bf16[2048,1024]{0,1:T(8,128)(2,1)} fusion(bf16[256,1024]{1,0:T(8,128)(2,1)S(1)} %bitcast.53, bf16[256,2048]{1,0:T(8,128)(2,1)} %bitcast.57), kind=kOutput, calls=%fused_computation.6 | convolution fusion | flops 1075838976 | bytes 5767168 | tf_op jit(solution)/shard_map/dot_general | solution.py:180
  128.2 3.3 %convert_bitcast_fusion.1 = bf16[2048,1024]{0,1:T(8,128)(2,1)} fusion(bf16[256,1024]{1,0:T(8,128)(2,1)S(1)} %bitcast.52, bf16[256,2048]{1,0:T(8,128)(2,1)S(1)} %bitcast.56), kind=kOutput, calls=%fused_computation.7 | convolution fusion | flops 1075838976 | bytes 5767168 | tf_op jit(solution)/shard_map/dot_general | solution.py:180
  131.5 13.2 %all-reduce.2.cloned.1.call-done = bf16[125,1024]{1,0:T(8,128)(2,1)} async-done(((bf16[125,1024]{1,0:T(8,128)(2,1)}), bf16[125,1024]{1,0:T(8,128)(2,1)}) %all-reduce.2.cloned.1.call-update) | async-done | bytes 256016 | tf_op jit(solution)/shard_map/psum | solution.py:216
  144.7 1.8 convert_element_type.75
  146.5 27.0 %reduce-scatter.5.cloned.1.call-done = bf16[1,4,4,16,512]{4,3,2,1,0:T(8,128)(2,1)} async-done(((bf16[1,4,4,16,2048]{4,3,2,1,0:T(8,128)(2,1)}), bf16[1,4,4,16,512]{4,3,2,1,0:T(8,128)(2,1)}) %reduce-scatter.5.cloned.1.call-update) | async-done | bytes 262160 | tf_op jit(solution)/shard_map/reduce_scatter | solution.py:171
  173.5 1.7 add_convert_fusion.1
  175.3 26.2 %reduce-scatter.7.cloned.1.call-done = bf16[1,4,4,16,512]{4,3,2,1,0:T(8,128)(2,1)} async-done(((bf16[1,4,4,16,2048]{4,3,2,1,0:T(8,128)(2,1)}), bf16[1,4,4,16,512]{4,3,2,1,0:T(8,128)(2,1)}) %reduce-scatter.7.cloned.1.call-update) | async-done | bytes 262160 | tf_op jit(solution)/shard_map/reduce_scatter | solution.py:171
  201.5 1.7 add_convert_fusion
  203.2 51.9 %reduce-scatter.11.cloned.1.call-done = bf16[256,1024]{0,1:T(8,128)(2,1)} async-done(((bf16[2048,1024]{0,1:T(8,128)(2,1)}), bf16[256,1024]{0,1:T(8,128)(2,1)}) %reduce-scatter.11.cloned.1.call-update) | async-done | bytes 524304 | tf_op jit(solution)/shard_map/reduce_scatter | solution.py:183
  255.1 2.0 copy.11
  257.1 52.7 %reduce-scatter.9.cloned.1.call-done = bf16[256,1024]{0,1:T(8,128)(2,1)} async-done(((bf16[2048,1024]{0,1:T(8,128)(2,1)}), bf16[256,1024]{0,1:T(8,128)(2,1)}) %reduce-scatter.9.cloned.1.call-update) | async-done | bytes 524304 | tf_op jit(solution)/shard_map/reduce_scatter | solution.py:183
  309.8 2.0 copy.10
  (29 shorter events, 0.6 us)
Async XLA Ops:
  7.2 33.1 %all-gather.3.cloned.1.call-start = ((), (), s32[]{:S(2)}) async-start(), calls=%async_computation.4 | async-start | bytes 1310720 | tf_op jit(solution)/shard_map/all_gather | solution.py:191
  7.9 69.7 %all-gather.5.cloned.1.call-start = ((), (), s32[]{:S(2)}) async-start(), calls=%async_computation.6 | async-start | bytes 1310720 | tf_op jit(solution)/shard_map/all_gather | solution.py:192
  40.2 15.1 %copy-start = (f32[125,1024]{1,0:T(8,128)S(1)}, f32[125,1024]{1,0:T(8,128)}, u32[]{:S(2)}) copy-start(f32[125,1024]{1,0:T(8,128)} %kernel.3) | copy-start | bytes 1536004
  44.1 11.1 %collective-permute-start.1 = (bf16[2,4,16,1024]{3,2,1,0:T(8,128)(2,1)S(1)}, bf16[2,4,16,1024]{3,2,1,0:T(8,128)(2,1)S(1)}, u32[]{:S(2)}, u32[]{:S(2)}) collective-permute-start(bf16[2,4,16,1024]{3,2,1,0:T(8,128)(2,1)S(1)} %bitcast.59), channel_id=1, source_target_pairs={{4,0},{8,4},{12,8},{5,1},{9,5},{13,9},{6,2},{10,6},{14,10},{7,3},{... | collective-permute-start | bytes 786440 | tf_op jit(solution)/shard_map/ppermute | solution.py:166
  45.4 9.8 %collective-permute-start = (bf16[2,4,16,1024]{3,2,1,0:T(8,128)(2,1)S(1)}, bf16[2,4,16,1024]{3,2,1,0:T(8,128)(2,1)S(1)}, u32[]{:S(2)}, u32[]{:S(2)}) collective-permute-start(bf16[2,4,16,1024]{3,2,1,0:T(8,128)(2,1)S(1)} %bitcast.58), channel_id=1, source_target_pairs={{0,4},{4,8},{8,12},{1,5},{5,9},{9,13},{2,6},{6,10},{10,14},{3,7},{... | collective-permute-start | bytes 786440 | tf_op jit(solution)/shard_map/ppermute | solution.py:165
  50.0 94.7 %all-reduce.2.cloned.1.call-start = ((), (), s32[]{:S(2)}) async-start(), calls=%async_computation.10 | async-start | bytes 524288 | tf_op jit(solution)/shard_map/psum | solution.py:216
  81.4 8.9 %copy-start.1 = (bf16[4,4,16,1024]{3,2,1,0:T(8,128)(2,1)S(1)}, bf16[4,4,16,1024]{3,2,1,0:T(8,128)(2,1)}, u32[]{:S(2)}) copy-start(bf16[4,4,16,1024]{3,2,1,0:T(8,128)(2,1)} %multiply_convert_fusion.1) | copy-start | bytes 1572868
  90.3 83.2 %reduce-scatter.5.cloned.1.call-start = ((), (), s32[]{:S(2)}) async-start(), calls=%async_computation.5 | async-start | bytes 1310720 | tf_op jit(solution)/shard_map/reduce_scatter | solution.py:171
  94.9 106.6 %reduce-scatter.7.cloned.1.call-start = ((), (), s32[]{:S(2)}) async-start(), calls=%async_computation.7 | async-start | bytes 1310720 | tf_op jit(solution)/shard_map/reduce_scatter | solution.py:171
  95.0 9.4 %collective-permute-start.2 = (bf16[2,4,16,1024]{3,2,1,0:T(8,128)(2,1)S(1)}, bf16[2,4,16,1024]{3,2,1,0:T(8,128)(2,1)S(1)}, u32[]{:S(2)}, u32[]{:S(2)}) collective-permute-start(bf16[2,4,16,1024]{3,2,1,0:T(8,128)(2,1)S(1)} %get-tuple-element.10), channel_id=1, source_target_pairs={{0,4},{4,8},{8,12},{1,5},{5,9},{9,13},{2,6},{6,10},{10,14},{3,7},{... | collective-permute-start | bytes 786440 | tf_op jit(solution)/shard_map/ppermute | solution.py:165
  98.4 13.5 %collective-permute-start.3 = (bf16[2,4,16,1024]{3,2,1,0:T(8,128)(2,1)S(1)}, bf16[2,4,16,1024]{3,2,1,0:T(8,128)(2,1)S(1)}, u32[]{:S(2)}, u32[]{:S(2)}) collective-permute-start(bf16[2,4,16,1024]{3,2,1,0:T(8,128)(2,1)S(1)} %get-tuple-element.11), channel_id=1, source_target_pairs={{4,0},{8,4},{12,8},{5,1},{9,5},{13,9},{6,2},{10,6},{14,10},{7,3},{... | collective-permute-start | bytes 786440 | tf_op jit(solution)/shard_map/ppermute | solution.py:166
  112.1 9.0 %copy-start.5 = (bf16[2048,1024]{1,0:T(8,128)(2,1)S(1)}, bf16[2048,1024]{1,0:T(8,128)(2,1)}, u32[]{:S(2)}) copy-start(bf16[2048,1024]{1,0:T(8,128)(2,1)} %param.6) | copy-start | bytes 12582916
  123.5 131.6 %reduce-scatter.11.cloned.1.call-start = ((), (), s32[]{:S(2)}) async-start(), calls=%async_computation.9 | async-start | bytes 4718592 | tf_op jit(solution)/shard_map/reduce_scatter | solution.py:183
  123.5 4.7 %copy-start.4 = (bf16[1,4,4,16,2048]{4,3,2,1,0:T(8,128)(2,1)S(1)}, bf16[1,4,4,16,2048]{4,3,2,1,0:T(8,128)(2,1)}, u32[]{:S(2)}) copy-start(bf16[1,4,4,16,2048]{4,3,2,1,0:T(8,128)(2,1)} %all-gather.3.cloned.1.call-done) | copy-start | bytes 3145732
  128.1 181.7 %reduce-scatter.9.cloned.1.call-start = ((), (), s32[]{:S(2)}) async-start(), calls=%async_computation.8 | async-start | bytes 4718592 | tf_op jit(solution)/shard_map/reduce_scatter | solution.py:183
  131.4 42.1 %copy-start.2 = (bf16[1,4,4,16,512]{4,3,2,1,0:T(8,128)(2,1)S(1)}, bf16[1,4,4,16,512]{4,3,2,1,0:T(8,128)(2,1)}, u32[]{:S(2)}) copy-start(bf16[1,4,4,16,512]{4,3,2,1,0:T(8,128)(2,1)} %param.5) | copy-start | bytes 786436
  131.5 70.1 %copy-start.3 = (bf16[1,4,4,16,512]{4,3,2,1,0:T(8,128)(2,1)S(1)}, bf16[1,4,4,16,512]{4,3,2,1,0:T(8,128)(2,1)}, u32[]{:S(2)}) copy-start(bf16[1,4,4,16,512]{4,3,2,1,0:T(8,128)(2,1)} %param.9) | copy-start | bytes 786436
Sparse Core Ops, SparseCore 0:
  9.6 30.6 all-gather.2
  50.1 27.3 all-gather.4
  90.5 54.2 all-reduce.1
  147.0 26.5 reduce-scatter.4
  175.7 25.7 reduce-scatter.6
  205.1 49.9 reduce-scatter.10
  258.5 51.3 reduce-scatter.8

commit v2 on v1

v2 whole, which is shorter than its diff:
```python
import functools

import jax
import jax.numpy as jnp
from jax import lax
from jax.experimental import pallas as pl
from jax.experimental.pallas import tpu as pltpu
from jax.sharding import PartitionSpec as P

LANES = 128
HALO = 2


def aligned(index, size):
    return pl.ds(pl.multiple_of(index * size, size), size)


def clear_windows(win):
    halves, depth, tile_x, _, lanes = win.shape
    zeros = jnp.zeros((8, lanes), jnp.float32)
    for z in range(depth):
        for x in range(tile_x):
            win[0, z, x, 0:8] = zeros
            win[halves - 1, z, x, 16:24] = zeros


def fill_windows(win, field, cols):
    halves, depth, tile_x, _, _ = win.shape
    tile_y = 8 * halves
    for z in range(depth):
        for x in range(tile_x):
            first_row = (z * tile_x + x) * tile_y
            line = field[first_row : first_row + tile_y, cols].astype(jnp.float32)
            for h in range(halves):
                for part in range(3):
                    first = 8 * (h + part - 1)
                    if 0 <= first < tile_y:
                        win[h, z, x, 8 * part : 8 * part + 8] = line[first : first + 8]


def pairs(source_z, source_x, planes, tile_x):
    for a in range(5):
        z = source_z - a
        if 0 <= z < planes:
            for b in range(5):
                x = source_x - b + 2
                if 0 <= x < tile_x:
                    yield a, b, z, x


def stencil_half(win, half, kernel, cols, mirror, planes, tile_x):
    accs = [[None] * tile_x for _ in range(planes)]
    for c in range(5):
        taps = {}
        for a in range(5):
            for b in range(5):
                t = 25 * a + 5 * b + c
                t = 124 - t if mirror else t
                taps[a, b] = jnp.broadcast_to(kernel[t : t + 1, cols], (8, LANES))
        for sz in range(planes + 2 * HALO):
            for sx in range(tile_x):
                cells = win[half, sz, sx, 6 + c : 14 + c]
                for a, b, z, x in pairs(sz, sx, planes, tile_x):
                    term = taps[a, b] * cells
                    accs[z][x] = term if accs[z][x] is None else accs[z][x] + term
    return accs


def stencil(win, field, kernel, mirror, planes, tile_x, wide, finish):
    halves = win.shape[0]
    tile_y = 8 * halves

    @pl.loop(0, kernel.shape[1] // LANES)
    def _(block):
        cols = aligned(block, LANES)
        fill_windows(win, field, cols)

        @pl.loop(0, halves)
        def _(half):
            accs = stencil_half(win, half, kernel, cols, mirror, planes, tile_x)
            for z in range(planes):
                for x in range(tile_x):
                    first = (z * tile_x + x) * tile_y + half * 8
                    wide[pl.ds(pl.multiple_of(first, 8), 8), cols] = accs[z][x]

        for line in range(planes * tile_x):
            rows = slice(line * tile_y, (line + 1) * tile_y)
            finish(rows, cols, wide[rows, cols])


def tap_sums(win, tmp, field, grad, out, planes, tile_x):
    halves = win.shape[0]
    tile_y = 8 * halves
    first_row = HALO * tile_x * tile_y

    @pl.loop(0, out.shape[1] // LANES)
    def _(block):
        cols = aligned(block, LANES)
        fill_windows(win, field, cols)
        for line in range(planes * tile_x):
            rows = slice(first_row + line * tile_y, first_row + (line + 1) * tile_y)
            tmp[line] = grad[rows, cols].astype(jnp.float32)
        for c in range(5):
            def one_half(half, sums):
                sums = list(sums)
                rows = aligned(half, 8)
                grads = [tmp[line, rows, :] for line in range(planes * tile_x)]
                for sz in range(planes + 2 * HALO):
                    for sx in range(tile_x):
                        cells = win[half, sz, sx, 6 + c : 14 + c]
                        for a, b, z, x in pairs(sz, sx, planes, tile_x):
                            sums[5 * a + b] = sums[5 * a + b] + cells * grads[z * tile_x + x]
                return tuple(sums)

            sums = lax.fori_loop(0, halves, one_half, (jnp.zeros((8, LANES), jnp.float32),) * 25)
            for ab in range(25):
                t = 5 * ab + c
                out[t : t + 1, cols] = jnp.sum(sums[ab], axis=0, keepdims=True)


def block_kernel(
    sizes, inputs, cotangent, up_weight, down_weight, kernel,
    block_output, input_grad, up_grad, down_grad, kernel_grad,
    xg, cg, upw, dnw, hid, grd, wide, act, hgr, win, tmp, sent, got, turned,
    first_out, first_in, second_out, second_in, taps, taps_out, taps_in, share_out, share_in, half_out, half_in,
    load_sem, ag_s, ag_r, halo_s, halo_r, rs_s, rs_r, pair_s, pair_r, row_s, row_r, kg_s, kg_r,
):
    planes, tile_x, tile_y, n_dp, n_row, n_col = sizes
    dp, row, col = lax.axis_index("dp"), lax.axis_index("row"), lax.axis_index("col")
    partner = {"dp": 1 - dp}
    voxels, local = inputs.shape
    channels = kernel.shape[1]
    plane = tile_x * tile_y
    own = slice(HALO * plane, HALO * plane + voxels)
    tile = min(256, channels)
    wtile = min(256, local)
    n_half = n_col // 2
    share = first_out.shape[1] * local // n_row
    bf16, f32 = jnp.bfloat16, jnp.float32
    mine = aligned(col, local)

    loads = [
        pltpu.make_async_copy(source, target, load_sem.at[i])
        for i, (source, target) in enumerate(
            ((inputs, xg.at[:, mine]), (up_weight, upw), (cotangent, cg.at[:, mine]), (down_weight, dnw))
        )
    ]
    for load in loads:
        load.start()

    barrier = pltpu.get_barrier_semaphore()

    @pl.loop(1, n_col)
    def _(k):
        pl.semaphore_signal(barrier, inc=1, device_id={"col": lax.rem(col + k, n_col)})

    @pl.loop(1, n_row)
    def _(k):
        pl.semaphore_signal(barrier, inc=1, device_id={"row": lax.rem(row + k, n_row)})

    pl.semaphore_signal(barrier, inc=1, device_id=partner)
    pl.semaphore_wait(barrier, n_col + n_row - 1)

    def remote(source, target, send, receive, device):
        return pltpu.make_async_remote_copy(
            src_ref=source, dst_ref=target, send_sem=send, recv_sem=receive,
            device_id=device, device_id_type=pl.DeviceIdType.MESH,
        )

    def gather(i, k):
        source, target = ((inputs, xg), (cotangent, cg))[i]
        return remote(
            source, target.at[:, mine], ag_s.at[i, k], ag_r.at[i, k], {"col": lax.rem(col + k, n_col)}
        )

    def each(count, action, first=1):
        @pl.loop(first, count)
        def _(k):
            action(k)

    each(n_col, lambda k: gather(0, k).start())
    each(n_col, lambda k: gather(0, k).wait_send())
    each(n_col, lambda k: gather(1, k).start())
    clear_windows(win)
    each(n_col, lambda k: gather(0, k).wait_recv())
    loads[0].wait()
    loads[1].wait()

    @pl.loop(0, channels // tile)
    def _(n):
        cols = aligned(n, tile)
        hid[own, cols] = jnp.dot(xg[...], upw[:, cols], preferred_element_type=f32).astype(bf16)

    def halo(i, field, side):
        if side:
            source, target, peer = field.at[HALO * plane : 2 * HALO * plane], voxels + HALO * plane, row - 1
        else:
            source, target, peer = field.at[voxels : voxels + HALO * plane], 0, row + 1
        return remote(
            source, field.at[target : target + HALO * plane], halo_s.at[i, side], halo_r.at[i, side], {"row": peer}
        )

    def halo_start(i, field):
        @pl.when(row < n_row - 1)
        def _():
            halo(i, field, 0).start()

        @pl.when(row > 0)
        def _():
            halo(i, field, 1).start()

        @pl.when(row == 0)
        def _():
            field[0 : HALO * plane] = jnp.zeros((HALO * plane, channels), bf16)

        @pl.when(row == n_row - 1)
        def _():
            field[voxels + HALO * plane :] = jnp.zeros((HALO * plane, channels), bf16)

    def halo_wait(i, field):
        @pl.when(row > 0)
        def _():
            halo(i, field, 0).wait_recv()
            halo(i, field, 1).wait_send()

        @pl.when(row < n_row - 1)
        def _():
            halo(i, field, 1).wait_recv()
            halo(i, field, 0).wait_send()

    halo_start(0, hid)
    halo_wait(0, hid)

    def activate(rows, cols, preact):
        act[rows, cols] = (preact * jax.nn.sigmoid(preact)).astype(bf16)

    stencil(win, hid, kernel, False, planes, tile_x, wide, activate)

    loads[2].wait()
    loads[3].wait()
    each(n_col, lambda k: gather(1, k).wait_recv())

    @pl.loop(0, channels // tile)
    def _(n):
        cols = aligned(n, tile)
        act_grad = jnp.dot(cg[...], dnw[:, cols], preferred_element_type=f32)
        preact = wide[:, cols]
        logistic = jax.nn.sigmoid(preact)
        grd[own, cols] = (act_grad * logistic * (1.0 + preact * (1.0 - logistic))).astype(bf16)

    halo_start(1, grd)

    def pair(i, j):
        return remote(first_out.at[i, j], first_in.at[i, j], pair_s.at[i, j], pair_r.at[i, j], partner)

    def turn(left, chunk):
        turned[...] = left[:, aligned(chunk, local)].T

    def grad_for_partner(i, left, right):
        @pl.loop(0, n_half)
        def _(j):
            turn(left, (1 - dp) * n_half + j)

            @pl.loop(0, channels // tile)
            def _(n):
                cols = aligned(n, tile)
                first_out[i, j, :, cols] = jnp.dot(
                    turned[...], right[:, cols], preferred_element_type=f32
                ).astype(bf16)

            pair(i, j).start()

    def row_copy(i, k):
        peer = lax.rem(row + k, n_row)
        return remote(
            second_out.at[i, aligned(peer, share)], second_in.at[i, k], row_s.at[i, k], row_r.at[i, k], {"row": peer}
        )

    def grad_own(i, left, right):
        @pl.loop(0, n_half)
        def _(j):
            turn(left, dp * n_half + j)
            pair(i, j).wait_recv()

            @pl.loop(0, channels // tile)
            def _(n):
                cols = aligned(n, tile)
                product = jnp.dot(turned[...], right[:, cols], preferred_element_type=f32).astype(bf16)
                both = product.astype(f32) + first_in[i, j, :, cols].astype(f32)
                second_out[i, aligned(j, local), cols] = both.astype(bf16)

        each(n_row, lambda k: row_copy(i, k).start())

    def grad_finish(i, out):
        each(n_row, lambda k: row_copy(i, k).wait_recv())

        @pl.loop(0, channels // tile)
        def _(n):
            cols = aligned(n, tile)
            total = second_out[i, aligned(row, share), cols].astype(f32)
            for k in range(1, n_row):
                total = total + second_in[i, k, :, cols].astype(f32)
            out[:, cols] = total.astype(bf16)

        each(n_row, lambda k: row_copy(i, k).wait_send())
        each(n_half, lambda j: pair(i, j).wait_send(), 0)

    def column_copy(i, k):
        return remote(sent.at[i, k], got.at[i, k], rs_s.at[i, k], rs_r.at[i, k], {"col": lax.rem(col + k, n_col)})

    def column_partials(i, left, weight):
        def one(k):
            first = lax.rem(col + k, n_col) * local

            @pl.loop(0, local // wtile)
            def _(n):
                rows = pl.ds(pl.multiple_of(first + n * wtile, wtile), wtile)
                product = lax.dot_general(
                    left[...], weight[rows, :], (((1,), (1,)), ((), ())), preferred_element_type=f32
                )
                sent[i, k, :, aligned(n, wtile)] = product.astype(bf16)

        @pl.loop(1, n_col)
        def _(k):
            one(k)
            column_copy(i, k).start()

        one(0)

    def column_finish(i, residual, out):
        each(n_col, lambda k: column_copy(i, k).wait_recv())
        total = sent[i, 0].astype(f32)
        for k in range(1, n_col):
            total = total + got[i, k].astype(f32)
        out[...] = (residual[:, mine].astype(f32) + total).astype(bf16)
        each(n_col, lambda k: column_copy(i, k).wait_send())

    column_partials(0, act, dnw)
    grad_for_partner(0, cg, act)

    tap_sums(win, tmp, hid, grd, taps, planes, tile_x)
    taps_out[0 : kernel.shape[0]] = taps[0 : kernel.shape[0]].astype(bf16)
    taps_out[kernel.shape[0] :] = jnp.zeros((taps_out.shape[0] - kernel.shape[0], channels), bf16)
    whole_taps = remote(taps_out, taps_in, kg_s.at[0], kg_r.at[0], partner)
    whole_taps.start()
    halo_wait(1, grd)
    grad_own(0, cg, act)

    def keep(rows, cols, total):
        hgr[rows, cols] = total.astype(bf16)

    stencil(win, grd, kernel, True, planes, tile_x, wide, keep)
    grad_for_partner(1, xg, hgr)
    column_partials(1, hgr, upw)
    grad_own(1, xg, hgr)

    whole_taps.wait_recv()
    some = aligned(dp, channels // 2)
    share_out[...] = (taps_out[:, some].astype(f32) + taps_in[:, some].astype(f32)).astype(bf16)

    def taps_copy(k):
        return remote(share_out, share_in.at[k], kg_s.at[k], kg_r.at[k], {"row": lax.rem(row + k, n_row)})

    each(n_row, lambda k: taps_copy(k).start())
    column_finish(0, xg, block_output)
    grad_finish(0, down_grad)
    each(n_row, lambda k: taps_copy(k).wait_recv())
    total = share_out[...].astype(f32)
    for k in range(1, n_row):
        total = total + share_in[k].astype(f32)
    half_out[...] = total
    halves = remote(half_out, half_in, kg_s.at[n_row], kg_r.at[n_row], partner)
    halves.start()
    kernel_grad[:, some] = half_out[0 : kernel.shape[0]]
    column_finish(1, cg, input_grad)
    halves.wait_recv()
    kernel_grad[:, aligned(1 - dp, channels // 2)] = half_in[0 : kernel.shape[0]]
    grad_finish(1, up_grad)
    each(n_col, lambda k: gather(1, k).wait_send())
    whole_taps.wait_send()
    each(n_row, lambda k: taps_copy(k).wait_send())
    halves.wait_send()


def on_device(inputs, up_weight, down_weight, kernel, cotangent):
    _, planes, tile_x, tile_y, local = inputs.shape
    n_dp, n_row, n_col = (lax.axis_size(name) for name in ("dp", "row", "col"))
    voxels = planes * tile_x * tile_y
    extended = voxels + 2 * HALO * tile_x * tile_y
    width, channels = up_weight.shape
    share = width // (n_dp * n_row)
    bf16, f32 = jnp.bfloat16, jnp.float32
    dma = pltpu.SemaphoreType.DMA
    taps = kernel.shape[0]
    tap_rows = -(-taps // 16) * 16
    vmem, anywhere = pl.BlockSpec(memory_space=pltpu.VMEM), pl.BlockSpec(memory_space=pl.ANY)
    outs = pl.pallas_call(
        functools.partial(block_kernel, (planes, tile_x, tile_y, n_dp, n_row, n_col)),
        out_shape=(
            jax.ShapeDtypeStruct((voxels, local), bf16),
            jax.ShapeDtypeStruct((voxels, local), bf16),
            jax.ShapeDtypeStruct((share, channels), bf16),
            jax.ShapeDtypeStruct((share, channels), bf16),
            jax.ShapeDtypeStruct((taps, channels), f32),
        ),
        in_specs=[anywhere] * 4 + [vmem],
        out_specs=(vmem,) * 5,
        scratch_shapes=[
            pltpu.VMEM((voxels, width), bf16),
            pltpu.VMEM((voxels, width), bf16),
            pltpu.VMEM((width, channels), bf16),
            pltpu.VMEM((width, channels), bf16),
            pltpu.VMEM((extended, channels), bf16),
            pltpu.VMEM((extended, channels), bf16),
            pltpu.VMEM((voxels, channels), f32),
            pltpu.VMEM((voxels, channels), bf16),
            pltpu.VMEM((voxels, channels), bf16),
            pltpu.VMEM((tile_y // 8, planes + 2 * HALO, tile_x, 24, LANES), f32),
            pltpu.VMEM((planes * tile_x, tile_y, LANES), f32),
            pltpu.VMEM((2, n_col, voxels, local), bf16),
            pltpu.VMEM((2, n_col, voxels, local), bf16),
            pltpu.VMEM((local, voxels), bf16),
            pltpu.VMEM((2, n_col // 2, local, channels), bf16),
            pltpu.VMEM((2, n_col // 2, local, channels), bf16),
            pltpu.VMEM((2, width // 2, channels), bf16),
            pltpu.VMEM((2, n_row, share, channels), bf16),
            pltpu.VMEM((tap_rows, channels), f32),
            pltpu.VMEM((tap_rows, channels), bf16),
            pltpu.VMEM((tap_rows, channels), bf16),
            pltpu.VMEM((tap_rows, channels // 2), bf16),
            pltpu.VMEM((n_row, tap_rows, channels // 2), bf16),
            pltpu.VMEM((tap_rows, channels // 2), f32),
            pltpu.VMEM((tap_rows, channels // 2), f32),
            dma((4,)),
            dma((2, n_col)), dma((2, n_col)),
            dma((2, 2)), dma((2, 2)),
            dma((2, n_col)), dma((2, n_col)),
            dma((2, n_col // 2)), dma((2, n_col // 2)),
            dma((2, n_row)), dma((2, n_row)),
            dma((n_row + 1,)), dma((n_row + 1,)),
        ],
        compiler_params=pltpu.CompilerParams(
            collective_id=0, has_side_effects=True, vmem_limit_bytes=56 << 20
        ),
    )(inputs.reshape(voxels, local), cotangent.reshape(voxels, local), up_weight, down_weight, kernel)
    return (outs[0].reshape(inputs.shape), outs[1].reshape(inputs.shape)) + tuple(outs[2:])


def solution(mesh):
    placed = (
        P("dp", "row", None, None, "col"),
        P(None, "col"),
        P(None, "col"),
        P(None, "col"),
        P("dp", "row", None, None, "col"),
    )
    return jax.shard_map(
        on_device,
        mesh=mesh,
        in_specs=placed,
        out_specs=(
            P("dp", "row", None, None, "col"),
            P("dp", "row", None, None, "col"),
            P(("dp", "row"), "col"),
            P(("dp", "row"), "col"),
            P(None, "col"),
        ),
        check_vma=False,
    )
```

time: 319 us -> 143 us (0.45)
  the two profiles are of different devices: /device:TPU:0 before, /device:TPU:9 now
where the time goes in v2:
time: 143 us; the launch traced here: 142 us
  Pallas kernels  133 us (93%)
  local copies, waits for them, and re-layouts  8.96 us (6%)
    pallas_call x1, Pallas kernels, on_device(): pl.pallas_call(functools.partial(block_kernel, (planes, tile_x, tile_y, n...  133 us
    unnamed x5, local copies, waits for them, and re-layouts  8.96 us

profile of v2, /device:TPU:9, one launch (start us, length us, event | category | flops | bytes accessed | tf_op | source)
XLA Modules:
  0.0 142.3 jit_solution(18159831062644539868)
XLA Ops:
  0.6 132.7 %shard_map.92 = (bf16[256,512]{1,0:T(8,128)(2,1)}, bf16[256,512]{1,0:T(8,128)(2,1)}, bf16[256,1024]{1,0:T(8,128)(2,1)}, bf16[256,1024]{1,0:T(8,128)(2,1)}, f32[125,1024]{1,0:T(8,128)}) custom-call(bf16[256,512]{1,0:T(8,128)(2,1)} %bitcast.4, bf16[256,512]{1,0:T(8,128)(2,1)} %bitcast.5, bf16[2048,1024]{1,0:T(8,128)(2,1)} %up_weight.1, ...), custom_call_target="tpu_custom_call" | custom-call | tf_op jit(solution)/shard_map/pallas_call | solution.py:397
  133.4 1.7 %copy.15 = bf16[1,4,4,16,512]{4,3,2,1,0:T(8,128)(2,1)} copy(bf16[1,4,4,16,512]{4,3,2,1,0:T(8,128)(2,1)} %bitcast.7) | data formatting | bytes 524288
  135.1 1.7 %copy.16 = bf16[1,4,4,16,512]{4,3,2,1,0:T(8,128)(2,1)} copy(bf16[1,4,4,16,512]{4,3,2,1,0:T(8,128)(2,1)} %bitcast.6) | data formatting | bytes 524288
  136.7 1.9 %copy.17 = bf16[256,1024]{1,0:T(8,128)(2,1)} copy(bf16[256,1024]{1,0:T(8,128)(2,1)} %get-tuple-element.22) | data formatting | bytes 1048576
  138.6 1.9 %copy.18 = bf16[256,1024]{1,0:T(8,128)(2,1)} copy(bf16[256,1024]{1,0:T(8,128)(2,1)} %get-tuple-element.23) | data formatting | bytes 1048576
  140.5 1.9 %copy.19 = f32[125,1024]{1,0:T(8,128)} copy(f32[125,1024]{1,0:T(8,128)} %get-tuple-element.24) | data formatting | bytes 1024000

commit v3 on v2

--- a/solution.py
+++ b/solution.py
@@ -66,7 +66,7 @@
     return accs
 
 
-def stencil(win, field, kernel, mirror, planes, tile_x, wide, finish):
+def stencil(win, field, kernel, mirror, planes, tile_x, wide, finish, midway=None):
     halves = win.shape[0]
     tile_y = 8 * halves
 
@@ -74,6 +74,8 @@
     def _(block):
         cols = aligned(block, LANES)
         fill_windows(win, field, cols)
+        if midway is not None:
+            pl.when(block == kernel.shape[1] // LANES // 2)(midway)
 
         @pl.loop(0, halves)
         def _(half):
@@ -119,9 +121,9 @@
 
 
 def block_kernel(
-    sizes, inputs, cotangent, up_weight, down_weight, kernel,
+    sizes, inputs, cotangent, up_weight, down_weight, stencil_weights,
     block_output, input_grad, up_grad, down_grad, kernel_grad,
-    xg, cg, upw, dnw, hid, grd, wide, act, hgr, win, tmp, sent, got, turned,
+    kernel, xg, cg, upw, dnw, hid, grd, wide, act, hgr, win, tmp, sent, got, turned,
     first_out, first_in, second_out, second_in, taps, taps_out, taps_in, share_out, share_in, half_out, half_in,
     load_sem, ag_s, ag_r, halo_s, halo_r, rs_s, rs_r, pair_s, pair_r, row_s, row_r, kg_s, kg_r,
 ):
@@ -142,7 +144,7 @@
     loads = [
         pltpu.make_async_copy(source, target, load_sem.at[i])
         for i, (source, target) in enumerate(
-            ((inputs, xg.at[:, mine]), (up_weight, upw), (cotangent, cg.at[:, mine]), (down_weight, dnw))
+            ((inputs, xg.at[:, mine]), (up_weight, upw), (stencil_weights, kernel), (cotangent, cg.at[:, mine]), (down_weight, dnw))
         )
     ]
     for load in loads:
@@ -167,22 +169,45 @@
             device_id=device, device_id_type=pl.DeviceIdType.MESH,
         )
 
-    def gather(i, k):
-        source, target = ((inputs, xg), (cotangent, cg))[i]
+    def hop(i, side, step):
+        gathered = (xg, cg)[i]
+        source = (inputs, cotangent)[i] if step == 0 else gathered.at[:, aligned(col - side * step, local)]
         return remote(
-            source, target.at[:, mine], ag_s.at[i, k], ag_r.at[i, k], {"col": lax.rem(col + k, n_col)}
+            source, gathered.at[:, aligned(col - side * step, local)],
+            ag_s.at[i, (side + 1) // 2, step], ag_r.at[i, (side + 1) // 2, step], {"col": col + side},
         )
+
+    def inside(index):
+        return jnp.logical_and(index >= 0, index < n_col)
+
+    def hop_start(i, step):
+        for side in (1, -1):
+            pl.when(jnp.logical_and(inside(col + side), inside(col - side * step)))(hop(i, side, step).start)
+
+    def hop_received(i, step):
+        for side in (1, -1):
+            pl.when(inside(col - side * (step + 1)))(hop(i, side, step).wait_recv)
+
+    def hop_sent(i, step):
+        for side in (1, -1):
+            pl.when(jnp.logical_and(inside(col + side), inside(col - side * step)))(hop(i, side, step).wait_send)
+
+    def advance(i, step):
+        if step < n_col - 1:
+            hop_received(i, step - 1)
+            hop_start(i, step)
 
     def each(count, action, first=1):
         @pl.loop(first, count)
         def _(k):
             action(k)
 
-    each(n_col, lambda k: gather(0, k).start())
-    each(n_col, lambda k: gather(0, k).wait_send())
-    each(n_col, lambda k: gather(1, k).start())
+    hop_start(0, 0)
     clear_windows(win)
-    each(n_col, lambda k: gather(0, k).wait_recv())
+    for step in range(1, n_col - 1):
+        advance(0, step)
+    hop_start(1, 0)
+    hop_received(0, n_col - 2)
     loads[0].wait()
     loads[1].wait()
 
@@ -190,6 +215,11 @@
     def _(n):
         cols = aligned(n, tile)
         hid[own, cols] = jnp.dot(xg[...], upw[:, cols], preferred_element_type=f32).astype(bf16)
+
+    def turn(i, left):
+        @pl.loop(0, n_col)
+        def _(chunk):
+            turned[i, aligned(chunk, local)] = left[:, aligned(chunk, local)].T
 
     def halo(i, field, side):
         if side:
@@ -229,16 +259,21 @@
             halo(i, field, 0).wait_send()
 
     halo_start(0, hid)
+    advance(1, 1)
+    turn(0, xg)
+    loads[2].wait()
     halo_wait(0, hid)
 
     def activate(rows, cols, preact):
         act[rows, cols] = (preact * jax.nn.sigmoid(preact)).astype(bf16)
 
-    stencil(win, hid, kernel, False, planes, tile_x, wide, activate)
-
-    loads[2].wait()
+    stencil(win, hid, kernel, False, planes, tile_x, wide, activate, lambda: advance(1, 2))
+
     loads[3].wait()
-    each(n_col, lambda k: gather(1, k).wait_recv())
+    loads[4].wait()
+    for step in range(3, n_col - 1):
+        advance(1, step)
+    hop_received(1, n_col - 2)
 
     @pl.loop(0, channels // tile)
     def _(n):
@@ -253,19 +288,16 @@
     def pair(i, j):
         return remote(first_out.at[i, j], first_in.at[i, j], pair_s.at[i, j], pair_r.at[i, j], partner)
 
-    def turn(left, chunk):
-        turned[...] = left[:, aligned(chunk, local)].T
-
-    def grad_for_partner(i, left, right):
+    def grad_for_partner(i, right):
         @pl.loop(0, n_half)
         def _(j):
-            turn(left, (1 - dp) * n_half + j)
+            chunk = aligned((1 - dp) * n_half + j, local)
 
             @pl.loop(0, channels // tile)
             def _(n):
                 cols = aligned(n, tile)
                 first_out[i, j, :, cols] = jnp.dot(
-                    turned[...], right[:, cols], preferred_element_type=f32
+                    turned[1 - i, chunk], right[:, cols], preferred_element_type=f32
                 ).astype(bf16)
 
             pair(i, j).start()
@@ -276,20 +308,23 @@
             second_out.at[i, aligned(peer, share)], second_in.at[i, k], row_s.at[i, k], row_r.at[i, k], {"row": peer}
         )
 
-    def grad_own(i, left, right):
+    def grad_own(i, right):
         @pl.loop(0, n_half)
         def _(j):
-            turn(left, dp * n_half + j)
+            chunk = aligned(dp * n_half + j, local)
             pair(i, j).wait_recv()
 
             @pl.loop(0, channels // tile)
             def _(n):
                 cols = aligned(n, tile)
-                product = jnp.dot(turned[...], right[:, cols], preferred_element_type=f32).astype(bf16)
+                product = jnp.dot(turned[1 - i, chunk], right[:, cols], preferred_element_type=f32).astype(bf16)
                 both = product.astype(f32) + first_in[i, j, :, cols].astype(f32)
                 second_out[i, aligned(j, local), cols] = both.astype(bf16)
 
-        each(n_row, lambda k: row_copy(i, k).start())
+            for part in range(local // share):
+                peer = j * (local // share) + part
+                k = lax.rem(peer - row + n_row, n_row)
+                pl.when(peer != row)(lambda: row_copy(i, k).start())
 
     def grad_finish(i, out):
         each(n_row, lambda k: row_copy(i, k).wait_recv())
@@ -335,25 +370,25 @@
         out[...] = (residual[:, mine].astype(f32) + total).astype(bf16)
         each(n_col, lambda k: column_copy(i, k).wait_send())
 
+    turn(1, cg)
+    grad_for_partner(0, act)
     column_partials(0, act, dnw)
-    grad_for_partner(0, cg, act)
-
+    grad_own(0, act)
+    halo_wait(1, grd)
+
+    def keep(rows, cols, total):
+        hgr[rows, cols] = total.astype(bf16)
+
+    stencil(win, grd, kernel, True, planes, tile_x, wide, keep)
+    grad_for_partner(1, hgr)
+    column_partials(1, hgr, upw)
+    grad_own(1, hgr)
     tap_sums(win, tmp, hid, grd, taps, planes, tile_x)
     taps_out[0 : kernel.shape[0]] = taps[0 : kernel.shape[0]].astype(bf16)
     taps_out[kernel.shape[0] :] = jnp.zeros((taps_out.shape[0] - kernel.shape[0], channels), bf16)
     whole_taps = remote(taps_out, taps_in, kg_s.at[0], kg_r.at[0], partner)
     whole_taps.start()
-    halo_wait(1, grd)
-    grad_own(0, cg, act)
-
-    def keep(rows, cols, total):
-        hgr[rows, cols] = total.astype(bf16)
-
-    stencil(win, grd, kernel, True, planes, tile_x, wide, keep)
-    grad_for_partner(1, xg, hgr)
-    column_partials(1, hgr, upw)
-    grad_own(1, xg, hgr)
-
+    column_finish(0, xg, block_output)
     whole_taps.wait_recv()
     some = aligned(dp, channels // 2)
     share_out[...] = (taps_out[:, some].astype(f32) + taps_in[:, some].astype(f32)).astype(bf16)
@@ -362,8 +397,8 @@
         return remote(share_out, share_in.at[k], kg_s.at[k], kg_r.at[k], {"row": lax.rem(row + k, n_row)})
 
     each(n_row, lambda k: taps_copy(k).start())
-    column_finish(0, xg, block_output)
     grad_finish(0, down_grad)
+    column_finish(1, cg, input_grad)
     each(n_row, lambda k: taps_copy(k).wait_recv())
     total = share_out[...].astype(f32)
     for k in range(1, n_row):
@@ -372,14 +407,24 @@
     halves = remote(half_out, half_in, kg_s.at[n_row], kg_r.at[n_row], partner)
     halves.start()
     kernel_grad[:, some] = half_out[0 : kernel.shape[0]]
-    column_finish(1, cg, input_grad)
+    grad_finish(1, up_grad)
     halves.wait_recv()
     kernel_grad[:, aligned(1 - dp, channels // 2)] = half_in[0 : kernel.shape[0]]
-    grad_finish(1, up_grad)
-    each(n_col, lambda k: gather(1, k).wait_send())
+    for i in range(2):
+        for step in range(n_col - 1):
+            hop_sent(i, step)
     whole_taps.wait_send()
     each(n_row, lambda k: taps_copy(k).wait_send())
     halves.wait_send()
+
+
+def hand_on(*refs):
+    done = refs[10]
+    copies = [pltpu.make_async_copy(refs[i], refs[5 + i], done.at[i]) for i in range(5)]
+    for copy in copies:
+        copy.start()
+    for copy in copies:
+        copy.wait()
 
 
 def on_device(inputs, up_weight, down_weight, kernel, cotangent):
@@ -403,9 +448,10 @@
             jax.ShapeDtypeStruct((share, channels), bf16),
             jax.ShapeDtypeStruct((taps, channels), f32),
         ),
-        in_specs=[anywhere] * 4 + [vmem],
+        in_specs=[anywhere] * 5,
         out_specs=(vmem,) * 5,
         scratch_shapes=[
+            pltpu.VMEM(kernel.shape, f32),
             pltpu.VMEM((voxels, width), bf16),
             pltpu.VMEM((voxels, width), bf16),
             pltpu.VMEM((width, channels), bf16),
@@ -419,7 +465,7 @@
             pltpu.VMEM((planes * tile_x, tile_y, LANES), f32),
             pltpu.VMEM((2, n_col, voxels, local), bf16),
             pltpu.VMEM((2, n_col, voxels, local), bf16),
-            pltpu.VMEM((local, voxels), bf16),
+            pltpu.VMEM((2, width, voxels), bf16),
             pltpu.VMEM((2, n_col // 2, local, channels), bf16),
             pltpu.VMEM((2, n_col // 2, local, channels), bf16),
             pltpu.VMEM((2, width // 2, channels), bf16),
@@ -431,8 +477,8 @@
             pltpu.VMEM((n_row, tap_rows, channels // 2), bf16),
             pltpu.VMEM((tap_rows, channels // 2), f32),
             pltpu.VMEM((tap_rows, channels // 2), f32),
-            dma((4,)),
-            dma((2, n_col)), dma((2, n_col)),
+            dma((5,)),
+            dma((2, 2, n_col)), dma((2, 2, n_col)),
             dma((2, 2)), dma((2, 2)),
             dma((2, n_col)), dma((2, n_col)),
             dma((2, n_col // 2)), dma((2, n_col // 2)),
@@ -443,6 +489,13 @@
             collective_id=0, has_side_effects=True, vmem_limit_bytes=56 << 20
         ),
     )(inputs.reshape(voxels, local), cotangent.reshape(voxels, local), up_weight, down_weight, kernel)
+    outs = pl.pallas_call(
+        hand_on,
+        out_shape=tuple(jax.ShapeDtypeStruct(out.shape, out.dtype) for out in outs),
+        in_specs=[anywhere] * 5,
+        out_specs=(anywhere,) * 5,
+        scratch_shapes=[dma((5,))],
+    )(*outs)
     return (outs[0].reshape(inputs.shape), outs[1].reshape(inputs.shape)) + tuple(outs[2:])
 
 

time: 143 us -> 180 us (1.26)
  the two profiles are of different devices: /device:TPU:9 before, /device:TPU:0 now
where the time goes in v3:
time: 180 us
  Pallas kernels  179 us (99%)
    pallas_call x1, Pallas kernels, on_device(): pl.pallas_call(functools.partial(block_kernel, (planes, tile_x, tile_y, n...  114 us
    pallas_call x1, Pallas kernels, on_device(): pl.pallas_call(hand_on, out_shape=tuple((jax.ShapeDtypeStruct(out.shape,...  64.7 us

profile of v3, /device:TPU:0, one launch (start us, length us, event | category | flops | bytes accessed | tf_op | source)
XLA Modules:
  0.0 179.8 jit_solution(1515954728039710700)
XLA Ops:
  0.6 114.5 %shard_map.92 = (bf16[256,512]{1,0:T(8,128)(2,1)}, bf16[256,512]{1,0:T(8,128)(2,1)}, bf16[256,1024]{1,0:T(8,128)(2,1)}, bf16[256,1024]{1,0:T(8,128)(2,1)}, f32[125,1024]{1,0:T(8,128)}) custom-call(bf16[256,512]{1,0:T(8,128)(2,1)} %bitcast.4, bf16[256,512]{1,0:T(8,128)(2,1)} %bitcast.5, bf16[2048,1024]{1,0:T(8,128)(2,1)} %up_weight.1, ...), custom_call_target="tpu_custom_call" | custom-call | tf_op jit(solution)/shard_map/pallas_call | solution.py:442
  115.1 64.7 %shard_map.93 = (bf16[256,512]{1,0:T(8,128)(2,1)}, bf16[256,512]{1,0:T(8,128)(2,1)}, bf16[256,1024]{1,0:T(8,128)(2,1)}, bf16[256,1024]{1,0:T(8,128)(2,1)}, f32[125,1024]{1,0:T(8,128)}) custom-call(bf16[256,512]{1,0:T(8,128)(2,1)} %get-tuple-element.15.refs_0_, bf16[256,512]{1,0:T(8,128)(2,1)} %get-tuple-element.16.refs_1_, ...), custom_call_target="tpu_custom_call" | custom-call | tf_op jit(solution)/shard_map/pallas_call | solution.py:492

commit v4 on v3

--- a/solution.py
+++ b/solution.py
@@ -419,12 +419,16 @@
 
 
 def hand_on(*refs):
-    done = refs[10]
-    copies = [pltpu.make_async_copy(refs[i], refs[5 + i], done.at[i]) for i in range(5)]
-    for copy in copies:
-        copy.start()
-    for copy in copies:
-        copy.wait()
+    arrived, done = refs[15], refs[16]
+    fetches = [pltpu.make_async_copy(refs[i], refs[10 + i], arrived.at[i]) for i in range(5)]
+    stores = [pltpu.make_async_copy(refs[10 + i], refs[5 + i], done.at[i]) for i in range(5)]
+    for fetch in fetches:
+        fetch.start()
+    for fetch, store in zip(fetches, stores):
+        fetch.wait()
+        store.start()
+    for store in stores:
+        store.wait()
 
 
 def on_device(inputs, up_weight, down_weight, kernel, cotangent):
@@ -494,7 +498,7 @@
         out_shape=tuple(jax.ShapeDtypeStruct(out.shape, out.dtype) for out in outs),
         in_specs=[anywhere] * 5,
         out_specs=(anywhere,) * 5,
-        scratch_shapes=[dma((5,))],
+        scratch_shapes=[pltpu.VMEM(out.shape, out.dtype) for out in outs] + [dma((5,)), dma((5,))],
     )(*outs)
     return (outs[0].reshape(inputs.shape), outs[1].reshape(inputs.shape)) + tuple(outs[2:])
 

time: 180 us -> 118 us (0.66)
  Pallas kernels: 179 us -> 117 us
    pallas_call x1, Pallas kernels: 64.7 us -> 2.43 us  [on_device(): pl.pallas_call(hand_on, out_shape=tuple((jax.ShapeDtypeStruct(out.shape,...]
where the time goes in v4:
time: 118 us
  Pallas kernels  117 us (99%)
    pallas_call x1, Pallas kernels, on_device(): pl.pallas_call(functools.partial(block_kernel, (planes, tile_x, tile_y, n...  114 us
    pallas_call x1, Pallas kernels, on_device(): pl.pallas_call(hand_on, out_shape=tuple((jax.ShapeDtypeStruct(out.shape,...  2.43 us

profile of v4, /device:TPU:0, one launch (start us, length us, event | category | flops | bytes accessed | tf_op | source)
XLA Modules:
  0.0 117.6 jit_solution(4455699052548277967)
XLA Ops:
  0.6 114.5 %shard_map.92 = (bf16[256,512]{1,0:T(8,128)(2,1)}, bf16[256,512]{1,0:T(8,128)(2,1)}, bf16[256,1024]{1,0:T(8,128)(2,1)}, bf16[256,1024]{1,0:T(8,128)(2,1)}, f32[125,1024]{1,0:T(8,128)}) custom-call(bf16[256,512]{1,0:T(8,128)(2,1)} %bitcast.4, bf16[256,512]{1,0:T(8,128)(2,1)} %bitcast.5, bf16[2048,1024]{1,0:T(8,128)(2,1)} %up_weight.1, ...), custom_call_target="tpu_custom_call" | custom-call | tf_op jit(solution)/shard_map/pallas_call | solution.py:446
  115.1 2.4 %shard_map.93 = (bf16[256,512]{1,0:T(8,128)(2,1)}, bf16[256,512]{1,0:T(8,128)(2,1)}, bf16[256,1024]{1,0:T(8,128)(2,1)}, bf16[256,1024]{1,0:T(8,128)(2,1)}, f32[125,1024]{1,0:T(8,128)}) custom-call(bf16[256,512]{1,0:T(8,128)(2,1)} %get-tuple-element.15.refs_0_, bf16[256,512]{1,0:T(8,128)(2,1)} %get-tuple-element.16.refs_1_, ...), custom_call_target="tpu_custom_call" | custom-call | tf_op jit(solution)/shard_map/pallas_call | solution.py:496
